TPU v7x, 256 devices: a whole 4x4x8 slice. The times are simulated.
256 devices in a mesh: gx: 16 (over z_lo, x), gy: 2 (over core), gz: 8 (over z_hi, y).
Axes of the slice: x: 4, y: 4, z: 8 (z_hi: 2, z_lo: 4; z = z_hi * 4 + z_lo), core: 2. Of those that a mesh axis runs over, the one named last changes fastest.
Arguments:
- tokens: bfloat16 [128, 32, 128, 192], P('gx', 'gy', 'gz'), may hold values from -6 to 6
- upstream: bfloat16 [128, 32, 128, 192], P('gx', 'gy', 'gz'), may hold values from -6 to 6
- norm_gain: float32 [192], replicated, may hold values from 0.25 to 1.75
- norm_bias: float32 [192], replicated, may hold values from -3 to 3
- qkv_weight: bfloat16 [192, 576], replicated, may hold values from -4 to 4, as said below
- qkv_bias: float32 [576], replicated, may hold values from -3 to 3
- proj_weight: bfloat16 [192, 192], replicated, may hold values from -0.4375 to 0.4375
Outputs:
- token_grad: bfloat16 [128, 32, 128, 192], P('gx', 'gy', 'gz')
- qkv_weight_grad: float32 [192, 576], replicated
- qkv_bias_grad: float32 [576], replicated
- proj_weight_grad: float32 [192, 192], replicated
- proj_bias_grad: float32 [192], replicated
- gain_grad: float32 [192], replicated
- norm_bias_grad: float32 [192], replicated
Inputs may be any that keep to these rules, and one draw needn't show every extreme that they name: `qkv_weight`: columns are the query, key and value projections in that order, each 6 heads of 32 columns.
All inputs are finite; a program needn't handle non-finite values.
Results may differ from a plain program's by a relative error of at most 0.02.
The roundings to bfloat16 on the way count: a program that leaves them out, or rounds other values in their place, can miss the bound.
Values may be sent and summed in bfloat16 or wider, within the bound.
No kernel may reach another device: no remote copies, remote signals or barrier semaphores. Data moves between devices by JAX's collectives and lax.ppermute only.
A program may use at most 64 MiB of HBM per device.

v0:
```python
import functools
import math

import jax
import jax.numpy as jnp
from jax import lax
from jax.experimental import pallas as pl
from jax.experimental.pallas import tpu as pltpu
from jax.sharding import Mesh, PartitionSpec as P

HEADS = 6
WIN = 8
SHIFT = 4
FAR = -1e30
LANES = 128
PARTS = 8
MAIN = 144
ROWS = MAIN + 8
BEGIN_AT = 3
STEPS_A = 1
STEPS_B = 2
FINISH_AT = 2
F32 = jnp.float32
BF16 = jnp.bfloat16


def dot(a, b):
    return jnp.dot(a, b, preferred_element_type=F32)


def dot_rows(a, b):
    return lax.dot_general(a, b, (((1,), (1,)), ((), ())), preferred_element_type=F32)


def dot_cols(a, b):
    return lax.dot_general(a, b, (((0,), (0,)), ((), ())), preferred_element_type=F32)


def window_kernel(
    flags, gain, nbias, w_cols, w_rows, qbias, proj, near, *rest, steps
):
    far = rest[:-8]
    out, grads, acc_qkv, acc_proj, acc_gain, acc_nb, packed_grad, attended = rest[-8:]
    width = w_rows.shape[0]
    count = WIN**3
    windows_here = near.shape[1] // WIN // steps
    step = pl.program_id(0)
    size = width // HEADS
    factor = size**-0.5
    scale = factor * math.log2(math.e)
    place = lax.broadcasted_iota(jnp.int32, (16, count), 1)
    row = lax.broadcasted_iota(jnp.int32, (16, count), 0)
    ones = jnp.ones((16, count), BF16)

    class Window:
        pass

    def begin(at):
        here = Window()
        here.at = at
        def gathered(lo, hi):
            pieces, start = [], 0
            for piece in far:
                first, last = max(lo - start, 0), min(hi - start, piece.shape[1])
                if first < last:
                    pieces.append(piece[:, first:last].astype(F32))
                start += piece.shape[1]
            return jnp.concatenate(pieces, axis=1)

        wide = windows_here * WIN
        received = gathered(at * WIN, (at + 1) * WIN)
        for j in range(1, steps):
            other = gathered(j * wide + at * WIN, j * wide + (at + 1) * WIN)
            received = jnp.where(step == j, other, received)
        own = near[:, pl.ds(step * wide + at * WIN, WIN)].astype(F32)
        arrived = jnp.concatenate([own, received], axis=0).reshape(count, 2 * width)
        here.upward = arrived[:, :width]
        here.upward_half = here.upward.astype(BF16)
        inputs = arrived[:, LANES:].T[width - LANES :]
        centred = inputs - jnp.mean(inputs, axis=0, keepdims=True)
        here.inverse = lax.rsqrt(jnp.mean(centred * centred, axis=0, keepdims=True) + 1e-5)
        here.normed = centred * here.inverse
        here.hidden = (here.normed * gain[...] + nbias[...]).astype(BF16)
        here.packed = (dot(w_cols[...], here.hidden) + qbias[...]).astype(BF16)
        here.att_grad = dot_rows(proj[...], here.upward_half).astype(BF16)
        last = jnp.where(step == steps - 1, flags[1], 0) if at == windows_here - 1 else 0
        code = (
            4 * flags[0] * ((place >> 8) & 1)
            + 2 * last * ((place >> 5) & 1)
            + flags[2] * ((place >> 2) & 1)
        )
        same = code == row
        here.query_code = jnp.where(same, 1.0, 0.0).astype(BF16)
        here.key_code = jnp.where(same, 0.0, FAR).astype(BF16)
        attended[at, width:, :] = ones
        return here

    def rows_of(kind, head):
        return slice(kind * width + size * head, kind * width + size * (head + 1))

    def score(here, head):
        return dot_cols(
            jnp.concatenate([here.packed[rows_of(1, head)], here.key_code], axis=0),
            jnp.concatenate([here.packed[rows_of(0, head)], here.query_code], axis=0),
        )

    def weigh(scores):
        peak = jnp.max(scores, axis=0, keepdims=True)
        return jnp.exp2((scores - peak) * scale).astype(BF16)

    def values(here, head):
        return jnp.concatenate([here.packed[rows_of(2, head)], ones], axis=0)

    def attend(here, head, expo):
        mixed = dot(values(here, head), expo)
        recip = 1.0 / mixed[size : size + 1]
        result = mixed[:size] * recip
        attended[here.at, rows_of(0, head), :] = result.astype(BF16)
        scaled = (here.att_grad[rows_of(0, head)].astype(F32) * recip).astype(BF16)
        inner = jnp.sum(scaled.astype(F32) * result, axis=0, keepdims=True)
        high = inner.astype(BF16).astype(F32)
        inner_rows = jnp.where(row == 0, -high, jnp.where(row == 1, high - inner, 0.0))
        return scaled, jnp.concatenate([scaled, inner_rows.astype(BF16)], axis=0)

    def pull_back(here, head, expo, scaled, spread):
        score_grad = expo * spread.astype(BF16)
        query, keyset = here.packed[rows_of(0, head)], here.packed[rows_of(1, head)]
        grad_of = packed_grad.at[here.at]
        grad_of[rows_of(2, head), :] = dot_rows(scaled, expo).astype(BF16)
        grad_of[rows_of(0, head), :] = (dot(keyset, score_grad) * factor).astype(BF16)
        grad_of[rows_of(1, head), :] = (dot_rows(score_grad, query).T * factor).astype(BF16)

    def add(total, value, at):
        if at == 0:
            value = jnp.where(step == 0, 0.0, total[...]) + value if steps > 1 else value
            total[...] = value
        else:
            total[...] = total[...] + value

    def finish(here):
        grad_half = packed_grad[here.at]
        add(
            acc_qkv,
            dot_rows(jnp.concatenate([here.hidden, ones], axis=0), grad_half),
            here.at,
        )
        add(acc_proj, dot(attended[here.at], here.upward_half), here.at)
        hidden_grad = dot(w_rows[...], grad_half)
        add(acc_gain, hidden_grad * here.normed, here.at)
        add(acc_nb, hidden_grad, here.at)
        normed_grad = hidden_grad * gain[...]
        first = jnp.mean(normed_grad, axis=0, keepdims=True)
        second = jnp.mean(normed_grad * here.normed, axis=0, keepdims=True)
        change = here.inverse * (normed_grad - first - here.normed * second)
        out[:, here.at * WIN : (here.at + 1) * WIN] = (
            (here.upward + change.T).reshape(WIN, WIN, WIN, width).astype(BF16)
        )

    heads = [(at, head) for at in range(windows_here) for head in range(HEADS)]
    begun = {0: begin(0)}
    scores, earlier = score(begun[0], 0), None
    for number in range(len(heads) + 1):
        inside = number < len(heads)
        at, head = heads[number] if inside else (windows_here, 0)
        if inside and head == BEGIN_AT and at + 1 < windows_here:
            begun[at + 1] = begin(at + 1)
        spread = None
        if earlier is not None:
            before, prior = begun[earlier[0]], earlier[1]
            spread = dot_cols(values(before, prior), earlier[4])
        following = None
        if number + 1 < len(heads):
            next_at, next_head = heads[number + 1]
            following = score(begun[next_at], next_head)
        expo = weigh(scores) if inside else None
        current = (at, head, expo, *attend(begun[at], head, expo)) if inside else None
        if earlier is not None:
            pull_back(before, prior, earlier[2], earlier[3], spread)
        if head == FINISH_AT and 0 < at < windows_here:
            finish(begun[at - 1])
        scores, earlier = following, current
    finish(begun[windows_here - 1])

    def put(at, value):
        done = 0
        while done < value.shape[0]:
            part, inside = divmod(at + done, MAIN)
            rows = min(value.shape[0] - done, MAIN - inside)
            grads[part, inside : inside + rows, :] = value[done : done + rows]
            done += rows

    def put_small(at, value):
        grads[at // 2, MAIN + at % 2, : value.shape[1]] = value[0]

    def over_tokens(value):
        folded = value[:, :LANES]
        for j in range(1, count // LANES):
            folded = folded + value[:, j * LANES : (j + 1) * LANES]
        return jnp.sum(folded.T, axis=0, keepdims=True)

    qkv = acc_qkv[...]
    prj = acc_proj[...]
    for j in range(4):
        put(width * j, qkv[:width, j * LANES : (j + 1) * LANES])
    put(width * 4, prj[:width, :LANES])
    put(
        width * 5,
        jnp.concatenate([qkv[:width, 4 * LANES :], prj[:width, LANES:]], axis=1),
    )
    grads[:, MAIN:, :] = jnp.zeros_like(grads[:, MAIN:, :])
    for j in range(5):
        put_small(j, qkv[width : width + 1, j * LANES : (j + 1) * LANES])
    small = [prj[width : width + 1], over_tokens(acc_gain[...]), over_tokens(acc_nb[...])]
    for j, value in enumerate(small):
        put_small(8 + 2 * j, value[:, :LANES])
        put_small(9 + 2 * j, value[:, LANES:])


def windows(steps, flags, weights, near, *far):
    depth, width_y, depth_z, wide = near.shape
    depth += far[0].shape[0]
    width = wide // 2
    count = WIN**3
    operands = (*weights, near, *far)
    return pl.pallas_call(
        functools.partial(window_kernel, steps=steps),
        grid=(steps,),
        in_specs=[pl.BlockSpec(memory_space=pltpu.SMEM)]
        + [pl.BlockSpec(memory_space=pltpu.VMEM)] * len(operands),
        out_specs=[
            pl.BlockSpec((depth, width_y // steps, depth_z, width), lambda i: (0, i, 0, 0)),
            pl.BlockSpec((PARTS, ROWS, LANES), lambda i: (0, 0, 0)),
        ],
        out_shape=[
            jax.ShapeDtypeStruct((depth, width_y, depth_z, width), BF16),
            jax.ShapeDtypeStruct((PARTS, ROWS, LANES), F32),
        ],
        scratch_shapes=[
            pltpu.VMEM((width + 16, 3 * width), F32),
            pltpu.VMEM((width + 16, width), F32),
            pltpu.VMEM((width, count), F32),
            pltpu.VMEM((width, count), F32),
            pltpu.VMEM((width_y // WIN // steps, 3 * width, count), BF16),
            pltpu.VMEM((width_y // WIN // steps, width + 16, count), BF16),
        ],
        compiler_params=pltpu.CompilerParams(vmem_limit_bytes=48 * 2**20),
        cost_estimate=pl.CostEstimate(
            flops=20 * 10**9, transcendentals=4 * 10**6, bytes_accessed=4 * 10**6
        ),
        name="window_grads",
    )(flags, *operands)


def swapped(value, axis, bit):
    axes = (axis,) if isinstance(axis, str) else axis
    count = math.prod(lax.axis_size(name) for name in axes)
    return lax.ppermute(value, axis, [(a, a ^ bit) for a in range(count)])


def coded(value):
    small = value[:, MAIN:]
    high = lax.reduce_precision(small, 8, 7)
    return jnp.concatenate([value[:, :MAIN], high, small - high], axis=1).astype(BF16)


def decoded(value):
    wide = value.astype(F32)
    small = wide[:, MAIN:ROWS] + wide[:, ROWS:]
    return jnp.concatenate([wide[:, :MAIN], small], axis=1)


def halve(value, axis):
    half = value.shape[0] // 2
    upper = lax.axis_index(axis) % 2
    kept = lax.dynamic_slice_in_dim(value, upper * half, half, 0)
    given = lax.dynamic_slice_in_dim(value, (1 - upper) * half, half, 0)
    return kept + decoded(swapped(coded(given), axis, 1))


def quarter(value, axis):
    part = value.shape[0] // 4
    at = lax.axis_index(axis)
    sent = coded(value)
    total = lax.dynamic_slice_in_dim(value, at * part, part, 0)
    for bits in (2, 1, 3):
        given = lax.dynamic_slice_in_dim(sent, (at ^ bits) * part, part, 0)
        total = total + decoded(swapped(given, axis, bits))
    return total


def sum_of_two(value, axes, bit):
    sent = coded(value)
    return decoded(sent) + decoded(swapped(sent, axes, bit))


def sum_of_four(value, axes, first, second):
    sent = coded(value)
    both = swapped(sent, axes, first ^ second)
    one, two = swapped(sent, axes, first), swapped(sent, axes, second)
    return (decoded(sent) + decoded(one)) + (decoded(two) + decoded(both))


def join_four(value, axis):
    at = lax.axis_index(axis)
    odd, upper = at % 2 == 1, at >= 2
    far, one, three = (swapped(value, axis, bits) for bits in (2, 1, 3))
    flat = [
        jnp.where(odd, one, value),
        jnp.where(odd, value, one),
        jnp.where(odd, three, far),
        jnp.where(odd, far, three),
    ]
    return jnp.concatenate([jnp.where(upper, flat[j ^ 2], flat[j]) for j in range(4)], axis=0)


def summed_everywhere(value):
    value = quarter(halve(value, "c"), "y")
    value = sum_of_four(value, ("x",), 1, 2)
    value = sum_of_two(value, ("zl", "zh"), 2)
    value = sum_of_four(value, ("zl", "zh"), 4, 1)
    return join_four(coded(value), "y")


def unpack_kernel(upper, mine, other, qkv, proj, qbias, pbias, gain, nbias, *, width, factor):
    here = upper[0] == 1
    first = decoded(jnp.where(here, other[...], mine[...])) * factor
    second = decoded(jnp.where(here, mine[...], other[...])) * factor
    both = jnp.concatenate([first, second], axis=0)
    main = both[:, :MAIN].reshape(PARTS * MAIN, LANES)
    block = lambda j: main[width * j : width * (j + 1)]
    for j in range(4):
        qkv[:, j * LANES : (j + 1) * LANES] = block(j)
    rest = block(5)
    qkv[:, 4 * LANES :] = rest[:, : width - LANES]
    proj[:, :LANES] = block(4)
    proj[:, LANES:] = rest[:, width - LANES :]

    def put(target, at):
        for j in range(-(-target.shape[0] // LANES)):
            wide = min(LANES, target.shape[0] - j * LANES)
            line = both[(at + j) // 2, MAIN + (at + j) % 2]
            target[j * LANES : j * LANES + wide] = line[:wide]

    for target, at in ((qbias, 0), (pbias, 8), (gain, 10), (nbias, 12)):
        put(target, at)


def unpacked(value, axis, width, factor):
    shapes = [(width, 3 * width), (width, width), (3 * width,), (width,), (width,), (width,)]
    return pl.pallas_call(
        functools.partial(unpack_kernel, width=width, factor=factor),
        in_specs=[pl.BlockSpec(memory_space=pltpu.SMEM)]
        + [pl.BlockSpec(memory_space=pltpu.VMEM)] * 2,
        out_specs=[pl.BlockSpec(memory_space=pltpu.VMEM)] * 6,
        out_shape=[jax.ShapeDtypeStruct(shape, F32) for shape in shapes],
        compiler_params=pltpu.CompilerParams(vmem_limit_bytes=16 * 2**20),
        name="unpack_sums",
    )(lax.axis_index(axis).reshape(1), value, swapped(value, axis, 1))


def passed_back(value, axes):
    sizes = [lax.axis_size(axis) for axis in axes]
    count = math.prod(sizes)
    return lax.ppermute(value, axes, [(a, (a - 1) % count) for a in range(count)])


def passed_back_both(value, first, second):
    ones = [lax.axis_size(axis) for axis in first]
    twos = [lax.axis_size(axis) for axis in second]
    n, m = math.prod(ones), math.prod(twos)
    pairs = [
        (a * m + b, ((a - 1) % n) * m + (b - 1) % m) for a in range(n) for b in range(m)
    ]
    return lax.ppermute(value, first + second, pairs)


def per_device(tokens, upstream, norm_gain, norm_bias, qkv_weight, qkv_bias, proj_weight):
    gx, gy, gz = ("zl", "x"), ("c",), ("zh", "y")
    width = tokens.shape[3]
    both = jnp.concatenate([upstream, tokens], axis=3)
    a_z, b_z = slice(SHIFT, SHIFT + WIN), slice(SHIFT + WIN, None)
    came_a = passed_back(both[:SHIFT, SHIFT:, a_z], gx)
    came_y = passed_back(both[:, :SHIFT], gy)
    came_ay = passed_back(came_y[:SHIFT, :, a_z], gx)
    both = jnp.concatenate([both[:, SHIFT:], came_y], axis=1)
    came_b = passed_back(both[:SHIFT, :, b_z], gx)
    came_z = passed_back(both[SHIFT:, :, :SHIFT], gz)
    came_xz = passed_back_both(both[:SHIFT, :, :SHIFT], gx, gz)
    def is_last(axes):
        at = jnp.int32(0)
        count = 1
        for axis in axes:
            at = at * lax.axis_size(axis) + lax.axis_index(axis)
            count *= lax.axis_size(axis)
        return (at == count - 1).astype(jnp.int32)

    last_x, last_y, last_z = is_last(gx), is_last(gy), is_last(gz)
    weights = (
        norm_gain.reshape(-1, 1),
        norm_bias.reshape(-1, 1),
        qkv_weight.T,
        qkv_weight,
        qkv_bias.reshape(-1, 1),
        proj_weight,
    )
    out_a, grads_a = windows(
        STEPS_A,
        jnp.stack([last_x, last_y, 0 * last_z]), weights, both[SHIFT:, :, a_z], came_a, came_ay
    )
    out_b, grads_b = windows(
        STEPS_B,
        jnp.stack([last_x, last_y, last_z]),
        weights,
        jnp.concatenate([both[SHIFT:, :, b_z], came_z], axis=2),
        jnp.concatenate([came_b, came_xz], axis=2),
    )
    token_grad = jnp.concatenate([out_a, out_b], axis=2)
    devices = math.prod(lax.axis_size(axis) for axis in gx + gy + gz)
    factor = float(math.prod(tokens.shape[:3]) * devices) ** (-0.5)
    quarters = summed_everywhere(grads_a + grads_b)
    qkv_grad, proj_grad, qbias_grad, pbias_grad, gain_grad, nbias_grad = unpacked(
        quarters, "c", width, factor
    )
    return (token_grad, qkv_grad, qbias_grad, proj_grad, pbias_grad, gain_grad, nbias_grad)


def solution(mesh):
    split = Mesh(mesh.devices.reshape(4, 4, 2, 2, 4), ("zl", "x", "c", "zh", "y"))
    block = P(("zl", "x"), "c", ("zh", "y"), None)
    return jax.shard_map(
        per_device,
        mesh=split,
        in_specs=(block, block, P(), P(), P(), P(), P()),
        out_specs=(block, P(), P(), P(), P(), P(), P()),
        check_vma=False,
    )
```

profile of v0, /device:TPU:1, one launch (start us, length us, event | category | flops | bytes accessed | tf_op | source)
XLA Modules:
  0.0 102.9 jit_solution(8471926578873493963)
XLA Ops:
  0.6 0.0 copy-start.3
  0.7 2.1 %fusion.2 = bf16[8,4,16,384]{3,2,1,0:T(8,128)(2,1)} fusion(bf16[8,16,16,192]{3,2,1,0:T(8,128)(2,1)} %param.8, bf16[8,16,16,192]{3,2,1,0:T(8,128)(2,1)} %param.7), kind=kLoop, calls=%fused_computation.15 | loop fusion | flops 786432 | bytes 1966080 | tf_op jit(solution)/shard_map/concatenate | solution.py:380
  2.7 3.2 %collective-permute-start = (bf16[8,4,16,384]{3,2,1,0:T(8,128)(2,1)}, bf16[8,4,16,384]{3,2,1,0:T(8,128)(2,1)S(1)}, u32[]{:S(2)}, u32[]{:S(2)}) collective-permute-start(bf16[8,4,16,384]{3,2,1,0:T(8,128)(2,1)} %fusion.2), channel_id=1, source_target_pairs={{0,8},{8,0},{1,9},{9,1},{2,10},{10,2},{3,11},{11,3},{4,12},{12,4},... | collective-permute-start | bytes 1179656 | tf_op jit(solution)/shard_map/ppermute | solution.py:364
  6.0 0.0 copy-done.2
  6.0 0.9 pad_maximum_fusion.3
  6.9 4.8 %collective-permute-start.1 = (bf16[4,12,8,384]{3,2,1,0:T(8,128)(2,1)}, bf16[4,12,8,384]{3,2,1,0:T(8,128)(2,1)S(1)}, u32[]{:S(2)}, u32[]{:S(2)}) collective-permute-start(bf16[4,12,8,384]{3,2,1,0:T(8,128)(2,1)} %pad_maximum_fusion.3), channel_id=1, source_target_pairs={{0,240},{16,0},{32,16},{48,32},{64,48},{80,64},{96,80},{112,96},{1... | collective-permute-start | bytes 884744 | tf_op jit(solution)/shard_map/ppermute | solution.py:364
  11.7 0.1 pad_add_fusion.2.flags
  11.8 1.7 %fusion = bf16[8,12,16,384]{3,2,1,0:T(8,128)(2,1)S(1)} fusion(bf16[8,16,16,192]{3,2,1,0:T(8,128)(2,1)S(1)} %copy-done.2, bf16[8,16,16,192]{3,2,1,0:T(8,128)(2,1)} %param.7), kind=kLoop, calls=%fused_computation.12 | loop fusion | flops 2359296 | bytes 2752512 | tf_op jit(solution)/shard_map/concatenate | solution.py:380
  13.5 0.1 pad_add_fusion.flags
  13.6 0.1 copy.16.gain
  13.7 0.0 copy-done.6
  13.7 0.1 copy.17.nbias
  13.9 0.1 reshape.545.qbias
  14.0 0.2 copy.15
  14.2 0.0 collective-permute-done
  14.2 0.6 collective-permute-start.2
  14.9 0.3 fusion.3
  15.2 0.0 copy-start.1
  15.2 0.3 collective-permute-start.4
  15.6 6.7 %collective-permute-start.3 = (bf16[4,16,4,384]{3,2,1,0:T(4,128)(2,1)S(1)}, bf16[4,16,4,384]{3,2,1,0:T(4,128)(2,1)S(1)}, u32[]{:S(2)}, u32[]{:S(2)}) collective-permute-start(bf16[4,16,4,384]{3,2,1,0:T(4,128)(2,1)S(1)} %get-tuple-element.35), channel_id=1, source_target_pairs={{0,7},{1,0},{2,1},{3,2},{4,3},{5,4},{6,5},{7,6},{8,15},{9,8},{10,9... | collective-permute-start | bytes 589832 | tf_op jit(solution)/shard_map/ppermute | solution.py:364
  22.2 0.0 collective-permute-start.5
  22.2 0.2 fusion.1.near
  22.4 0.0 collective-permute-done.1.rest_0_
  22.4 0.0 collective-permute-done.2.rest_1_
  22.4 12.0 %window_grads.2 = (bf16[8,16,8,192]{3,2,1,0:T(8,128)(2,1)S(1)}, f32[8,152,128]{2,1,0:T(8,128)S(1)}) custom-call(s32[3]{0:T(128)S(1)} %pad_add_fusion.flags, f32[192,1]{1,0:T(8,128)S(1)} %copy.16.gain, f32[192,1]{1,0:T(8,128)S(1)} %copy.17.nbias, bf16[576,192]{1,0:T(8,128)(2,1)S(1)} %bitcast.7, bf16[192,576]{1,0:T(8,128)(2,1)S(1)} %copy-done, ...), custom_call_target="tpu_custom_call" | custom-call | flops 20000000000 | bytes 4000000 | tf_op jit(solution)/shard_map/window_grads/pallas_call | solution.py:225
  34.4 10.4 %collective-permute-done.3 = bf16[4,16,4,384]{3,2,1,0:T(4,128)(2,1)S(1)} collective-permute-done((bf16[4,16,4,384]{3,2,1,0:T(4,128)(2,1)S(1)}, bf16[4,16,4,384]{3,2,1,0:T(4,128)(2,1)S(1)}, u32[]{:S(2)}, u32[]{:S(2)}) %collective-permute-start.3) | collective-permute-done | bytes 196640 | tf_op jit(solution)/shard_map/ppermute | solution.py:364
  44.8 0.2 pad_maximum_fusion.1.near
  45.0 0.0 collective-permute-done.4
  45.1 0.0 collective-permute-done.5
  45.1 0.2 pad_maximum_fusion.2.rest_0_
  45.3 13.4 %window_grads.3 = (bf16[8,16,8,192]{3,2,1,0:T(8,128)(2,1)S(1)}, f32[8,152,128]{2,1,0:T(8,128)S(1)}) custom-call(s32[3]{0:T(128)S(1)} %pad_add_fusion.2.flags, f32[192,1]{1,0:T(8,128)S(1)} %copy.16.gain, f32[192,1]{1,0:T(8,128)S(1)} %copy.17.nbias, bf16[576,192]{1,0:T(8,128)(2,1)S(1)} %bitcast.8, bf16[192,576]{1,0:T(8,128)(2,1)S(1)} %copy-done, ...), custom_call_target="tpu_custom_call" | custom-call | flops 20000000000 | bytes 4000000 | tf_op jit(solution)/shard_map/window_grads/pallas_call | solution.py:225
  58.7 0.1 add.168
  58.9 0.9 collective-permute-start.6
  59.8 1.0 collective-permute-done.6
  61.0 0.1 collective-permute-start.7
  61.1 4.2 %collective-permute-start.9 = (bf16[1,160,128]{2,1,0:T(8,128)(2,1)S(1)}, bf16[1,160,128]{2,1,0:T(8,128)(2,1)S(1)}, u32[]{:S(2)}, u32[]{:S(2)}) collective-permute-start(bf16[1,160,128]{2,1,0:T(8,128)(2,1)S(1)} %get-tuple-element.45), channel_id=1, source_target_pairs={{0,3},{1,2},{2,1},{3,0},{4,7},{5,6},{6,5},{7,4},{8,11},{9,10},{10,... | collective-permute-start | bytes 122888 | tf_op jit(solution)/shard_map/ppermute | solution.py:257
  65.3 0.5 collective-permute-start.8
  65.8 0.0 collective-permute-done.7
  65.8 2.6 %collective-permute-done.8 = bf16[1,160,128]{2,1,0:T(8,128)(2,1)S(1)} collective-permute-done((bf16[1,160,128]{2,1,0:T(8,128)(2,1)S(1)}, bf16[1,160,128]{2,1,0:T(8,128)(2,1)S(1)}, u32[]{:S(2)}, u32[]{:S(2)}) %collective-permute-start.8) | collective-permute-done | bytes 40992 | tf_op jit(solution)/shard_map/ppermute | solution.py:257
  68.4 0.0 collective-permute-done.9
  68.6 0.1 collective-permute-start.12
  68.7 0.1 collective-permute-start.11
  68.8 3.2 %collective-permute-start.10 = (bf16[1,160,128]{2,1,0:T(8,128)(2,1)S(1)}, bf16[1,160,128]{2,1,0:T(8,128)(2,1)S(1)}, u32[]{:S(2)}, u32[]{:S(2)}) collective-permute-start(bf16[1,160,128]{2,1,0:T(8,128)(2,1)S(1)} %get-tuple-element.55), channel_id=1, source_target_pairs={{0,16},{16,0},{32,48},{48,32},{1,17},{17,1},{33,49},{49,33},{2,18}... | collective-permute-start | bytes 122888 | tf_op jit(solution)/shard_map/ppermute | solution.py:257
  72.0 0.7 collective-permute-done.12
  72.8 1.1 %collective-permute-done.10 = bf16[1,160,128]{2,1,0:T(8,128)(2,1)S(1)} collective-permute-done((bf16[1,160,128]{2,1,0:T(8,128)(2,1)S(1)}, bf16[1,160,128]{2,1,0:T(8,128)(2,1)S(1)}, u32[]{:S(2)}, u32[]{:S(2)}) %collective-permute-start.10) | collective-permute-done | bytes 40992 | tf_op jit(solution)/shard_map/ppermute | solution.py:257
  73.9 0.0 collective-permute-done.11
  74.1 0.1 collective-permute-start.13
  74.2 2.8 %collective-permute-done.13 = bf16[1,160,128]{2,1,0:T(8,128)(2,1)S(1)} collective-permute-done((bf16[1,160,128]{2,1,0:T(8,128)(2,1)S(1)}, bf16[1,160,128]{2,1,0:T(8,128)(2,1)S(1)}, u32[]{:S(2)}, u32[]{:S(2)}) %collective-permute-start.13) | collective-permute-done | bytes 40992 | tf_op jit(solution)/shard_map/ppermute | solution.py:257
  77.1 0.1 collective-permute-start.16
  77.2 5.9 %collective-permute-start.15 = (bf16[1,160,128]{2,1,0:T(8,128)(2,1)S(1)}, bf16[1,160,128]{2,1,0:T(8,128)(2,1)S(1)}, u32[]{:S(2)}, u32[]{:S(2)}) collective-permute-start(bf16[1,160,128]{2,1,0:T(8,128)(2,1)S(1)} %get-tuple-element.51), channel_id=1, source_target_pairs={{0,4},{4,0},{64,68},{68,64},{128,132},{132,128},{192,196},{196,192... | collective-permute-start | bytes 122888 | tf_op jit(solution)/shard_map/ppermute | solution.py:257
  83.1 0.0 collective-permute-start.14
  83.1 0.0 collective-permute-done.16
  83.1 4.0 %collective-permute-done.14 = bf16[1,160,128]{2,1,0:T(8,128)(2,1)S(1)} collective-permute-done((bf16[1,160,128]{2,1,0:T(8,128)(2,1)S(1)}, bf16[1,160,128]{2,1,0:T(8,128)(2,1)S(1)}, u32[]{:S(2)}, u32[]{:S(2)}) %collective-permute-start.14) | collective-permute-done | bytes 40992 | tf_op jit(solution)/shard_map/ppermute | solution.py:257
  87.2 0.0 collective-permute-done.15
  87.3 0.6 collective-permute-start.19
  87.9 1.7 %collective-permute-start.18 = (bf16[1,160,128]{2,1,0:T(8,128)(2,1)S(1)}, bf16[1,160,128]{2,1,0:T(8,128)(2,1)S(1)}, u32[]{:S(2)}, u32[]{:S(2)}) collective-permute-start(bf16[1,160,128]{2,1,0:T(8,128)(2,1)S(1)} %pad_maximum_fusion.11), channel_id=1, source_target_pairs={{0,2},{1,3},{2,0},{3,1},{4,6},{5,7},{6,4},{7,5},{8,10},{9,11},{10,... | collective-permute-start | bytes 122888 | tf_op jit(solution)/shard_map/ppermute | solution.py:257
  89.6 1.7 %collective-permute-start.17 = (bf16[1,160,128]{2,1,0:T(8,128)(2,1)S(1)}, bf16[1,160,128]{2,1,0:T(8,128)(2,1)S(1)}, u32[]{:S(2)}, u32[]{:S(2)}) collective-permute-start(bf16[1,160,128]{2,1,0:T(8,128)(2,1)S(1)} %pad_maximum_fusion.11), channel_id=1, source_target_pairs={{0,3},{1,2},{2,1},{3,0},{4,7},{5,6},{6,5},{7,4},{8,11},{9,10},{10,... | collective-permute-start | bytes 122888 | tf_op jit(solution)/shard_map/ppermute | solution.py:257
  91.3 0.0 collective-permute-done.19
  91.3 1.0 collective-permute-done.18
  92.2 1.4 %collective-permute-done.17 = bf16[1,160,128]{2,1,0:T(8,128)(2,1)S(1)} collective-permute-done((bf16[1,160,128]{2,1,0:T(8,128)(2,1)S(1)}, bf16[1,160,128]{2,1,0:T(8,128)(2,1)S(1)}, u32[]{:S(2)}, u32[]{:S(2)}) %collective-permute-start.17) | collective-permute-done | bytes 40992 | tf_op jit(solution)/shard_map/ppermute | solution.py:257
  93.7 7.0 %collective-permute-start.20 = (bf16[4,160,128]{2,1,0:T(8,128)(2,1)S(1)}, bf16[4,160,128]{2,1,0:T(8,128)(2,1)S(1)}, u32[]{:S(2)}, u32[]{:S(2)}) collective-permute-start(bf16[4,160,128]{2,1,0:T(8,128)(2,1)S(1)} %pad_maximum_fusion.7.mine), channel_id=1, source_target_pairs={{0,8},{8,0},{1,9},{9,1},{2,10},{10,2},{3,11},{11,3},{4,12},{12,4},... | collective-permute-start | bytes 491528 | tf_op jit(solution)/shard_map/ppermute | solution.py:257
  100.7 1.2 %pad_maximum_fusion = bf16[8,16,16,192]{3,2,1,0:T(8,128)(2,1)} fusion(bf16[8,16,8,192]{3,2,1,0:T(8,128)(2,1)S(1)} %get-tuple-element.18, bf16[8,16,8,192]{3,2,1,0:T(8,128)(2,1)S(1)} %get-tuple-element.17), kind=kLoop, calls=%fused_computation.13 | loop fusion | flops 1572864 | bytes 1572864 | tf_op jit(solution)/shard_map/concatenate | solution.py:417
  101.9 0.0 collective-permute-done.20.other
  101.9 0.9 unpack_sums.1
  (79 shorter events, 0.8 us)
Async XLA Ops:
  0.6 5.3 %copy-start.2 = (bf16[8,16,16,192]{3,2,1,0:T(8,128)(2,1)S(1)}, bf16[8,16,16,192]{3,2,1,0:T(8,128)(2,1)}, u32[]{:S(2)}) copy-start(bf16[8,16,16,192]{3,2,1,0:T(8,128)(2,1)} %param.8) | copy-start | bytes 2359300
  0.6 5.3 %copy-start.3 = (bf16[8,16,16,192]{3,2,1,0:T(8,128)(2,1)S(1)}, bf16[8,16,16,192]{3,2,1,0:T(8,128)(2,1)}, u32[]{:S(2)}) copy-start(bf16[8,16,16,192]{3,2,1,0:T(8,128)(2,1)} %param.7) | copy-start | bytes 2359300
  2.7 11.4 %collective-permute-start = (bf16[8,4,16,384]{3,2,1,0:T(8,128)(2,1)}, bf16[8,4,16,384]{3,2,1,0:T(8,128)(2,1)S(1)}, u32[]{:S(2)}, u32[]{:S(2)}) collective-permute-start(bf16[8,4,16,384]{3,2,1,0:T(8,128)(2,1)} %fusion.2), channel_id=1, source_target_pairs={{0,8},{8,0},{1,9},{9,1},{2,10},{10,2},{3,11},{11,3},{4,12},{12,4},... | collective-permute-start | bytes 1179656 | tf_op jit(solution)/shard_map/ppermute | solution.py:364
  6.9 15.5 %collective-permute-start.1 = (bf16[4,12,8,384]{3,2,1,0:T(8,128)(2,1)}, bf16[4,12,8,384]{3,2,1,0:T(8,128)(2,1)S(1)}, u32[]{:S(2)}, u32[]{:S(2)}) collective-permute-start(bf16[4,12,8,384]{3,2,1,0:T(8,128)(2,1)} %pad_maximum_fusion.3), channel_id=1, source_target_pairs={{0,240},{16,0},{32,16},{48,32},{64,48},{80,64},{96,80},{112,96},{1... | collective-permute-start | bytes 884744 | tf_op jit(solution)/shard_map/ppermute | solution.py:364
  11.8 1.8 %copy-start.5 = (f32[192]{0:T(256)S(1)}, f32[192]{0:T(256)}, u32[]{:S(2)}) copy-start(f32[192]{0:T(256)} %param.9) | copy-start | bytes 2308
  11.8 1.9 %copy-start.6 = (f32[192]{0:T(256)S(1)}, f32[192]{0:T(256)}, u32[]{:S(2)}) copy-start(f32[192]{0:T(256)} %param.10) | copy-start | bytes 2308
  11.8 2.1 %copy-start.4 = (f32[576]{0:T(1024)S(1)}, f32[576]{0:T(1024)}, u32[]{:S(2)}) copy-start(f32[576]{0:T(1024)} %param.12) | copy-start | bytes 6916
  11.8 2.2 %copy-start = (bf16[192,576]{1,0:T(8,128)(2,1)S(1)}, bf16[192,576]{1,0:T(8,128)(2,1)}, u32[]{:S(2)}) copy-start(bf16[192,576]{1,0:T(8,128)(2,1)} %w_rows.3) | copy-start | bytes 663556
  14.2 8.2 %collective-permute-start.2 = (bf16[4,4,8,384]{3,2,1,0:T(8,128)(2,1)S(1)}, bf16[4,4,8,384]{3,2,1,0:T(8,128)(2,1)S(1)}, u32[]{:S(2)}, u32[]{:S(2)}) collective-permute-start(bf16[4,4,8,384]{3,2,1,0:T(8,128)(2,1)S(1)} %slice.264), channel_id=1, source_target_pairs={{0,240},{16,0},{32,16},{48,32},{64,48},{80,64},{96,80},{112,96},{1... | collective-permute-start | bytes 294920 | tf_op jit(solution)/shard_map/ppermute | solution.py:364
  15.2 7.2 %copy-start.1 = (bf16[192,192]{1,0:T(8,128)(2,1)S(1)}, bf16[192,192]{1,0:T(8,128)(2,1)}, u32[]{:S(2)}) copy-start(bf16[192,192]{1,0:T(8,128)(2,1)} %proj.3) | copy-start | bytes 221188
  15.2 29.8 %collective-permute-start.4 = (bf16[4,16,4,384]{3,2,1,0:T(4,128)(2,1)S(1)}, bf16[4,16,4,384]{3,2,1,0:T(4,128)(2,1)S(1)}, u32[]{:S(2)}, u32[]{:S(2)}) collective-permute-start(bf16[4,16,4,384]{3,2,1,0:T(4,128)(2,1)S(1)} %get-tuple-element.33), channel_id=1, source_target_pairs={{0,240},{16,0},{32,16},{48,32},{64,48},{80,64},{96,80},{112,96},{1... | collective-permute-start | bytes 589832 | tf_op jit(solution)/shard_map/ppermute | solution.py:364
  15.6 29.3 %collective-permute-start.3 = (bf16[4,16,4,384]{3,2,1,0:T(4,128)(2,1)S(1)}, bf16[4,16,4,384]{3,2,1,0:T(4,128)(2,1)S(1)}, u32[]{:S(2)}, u32[]{:S(2)}) collective-permute-start(bf16[4,16,4,384]{3,2,1,0:T(4,128)(2,1)S(1)} %get-tuple-element.35), channel_id=1, source_target_pairs={{0,7},{1,0},{2,1},{3,2},{4,3},{5,4},{6,5},{7,6},{8,15},{9,8},{10,9... | collective-permute-start | bytes 589832 | tf_op jit(solution)/shard_map/ppermute | solution.py:364
  22.2 22.8 %collective-permute-start.5 = (bf16[4,16,4,384]{3,2,1,0:T(4,128)(2,1)S(1)}, bf16[4,16,4,384]{3,2,1,0:T(4,128)(2,1)S(1)}, u32[]{:S(2)}, u32[]{:S(2)}) collective-permute-start(bf16[4,16,4,384]{3,2,1,0:T(4,128)(2,1)S(1)} %get-tuple-element.36), channel_id=1, source_target_pairs={{0,247},{1,240},{2,241},{3,242},{4,243},{5,244},{6,245},{7,246},{1... | collective-permute-start | bytes 589832 | tf_op jit(solution)/shard_map/ppermute | solution.py:374
  58.9 1.9 %collective-permute-start.6 = (bf16[4,160,128]{2,1,0:T(8,128)(2,1)S(1)}, bf16[4,160,128]{2,1,0:T(8,128)(2,1)S(1)}, u32[]{:S(2)}, u32[]{:S(2)}) collective-permute-start(bf16[4,160,128]{2,1,0:T(8,128)(2,1)S(1)} %pad_maximum_fusion.5), channel_id=1, source_target_pairs={{0,8},{8,0},{1,9},{9,1},{2,10},{10,2},{3,11},{11,3},{4,12},{12,4},... | collective-permute-start | bytes 491528 | tf_op jit(solution)/shard_map/ppermute | solution.py:257
  61.0 4.8 %collective-permute-start.7 = (bf16[1,160,128]{2,1,0:T(8,128)(2,1)S(1)}, bf16[1,160,128]{2,1,0:T(8,128)(2,1)S(1)}, u32[]{:S(2)}, u32[]{:S(2)}) collective-permute-start(bf16[1,160,128]{2,1,0:T(8,128)(2,1)S(1)} %get-tuple-element.47), channel_id=1, source_target_pairs={{0,2},{1,3},{2,0},{3,1},{4,6},{5,7},{6,4},{7,5},{8,10},{9,11},{10,... | collective-permute-start | bytes 122888 | tf_op jit(solution)/shard_map/ppermute | solution.py:257
  61.1 7.3 %collective-permute-start.9 = (bf16[1,160,128]{2,1,0:T(8,128)(2,1)S(1)}, bf16[1,160,128]{2,1,0:T(8,128)(2,1)S(1)}, u32[]{:S(2)}, u32[]{:S(2)}) collective-permute-start(bf16[1,160,128]{2,1,0:T(8,128)(2,1)S(1)} %get-tuple-element.45), channel_id=1, source_target_pairs={{0,3},{1,2},{2,1},{3,0},{4,7},{5,6},{6,5},{7,4},{8,11},{9,10},{10,... | collective-permute-start | bytes 122888 | tf_op jit(solution)/shard_map/ppermute | solution.py:257
  65.3 3.1 %collective-permute-start.8 = (bf16[1,160,128]{2,1,0:T(8,128)(2,1)S(1)}, bf16[1,160,128]{2,1,0:T(8,128)(2,1)S(1)}, u32[]{:S(2)}, u32[]{:S(2)}) collective-permute-start(bf16[1,160,128]{2,1,0:T(8,128)(2,1)S(1)} %get-tuple-element.46), channel_id=1, source_target_pairs={{0,1},{1,0},{2,3},{3,2},{4,5},{5,4},{6,7},{7,6},{8,9},{9,8},{10,11... | collective-permute-start | bytes 122888 | tf_op jit(solution)/shard_map/ppermute | solution.py:257
  68.6 4.2 %collective-permute-start.12 = (bf16[1,160,128]{2,1,0:T(8,128)(2,1)S(1)}, bf16[1,160,128]{2,1,0:T(8,128)(2,1)S(1)}, u32[]{:S(2)}, u32[]{:S(2)}) collective-permute-start(bf16[1,160,128]{2,1,0:T(8,128)(2,1)S(1)} %get-tuple-element.55), channel_id=1, source_target_pairs={{0,48},{16,32},{32,16},{48,0},{1,49},{17,33},{33,17},{49,1},{2,50}... | collective-permute-start | bytes 122888 | tf_op jit(solution)/shard_map/ppermute | solution.py:257
  68.7 5.2 %collective-permute-start.11 = (bf16[1,160,128]{2,1,0:T(8,128)(2,1)S(1)}, bf16[1,160,128]{2,1,0:T(8,128)(2,1)S(1)}, u32[]{:S(2)}, u32[]{:S(2)}) collective-permute-start(bf16[1,160,128]{2,1,0:T(8,128)(2,1)S(1)} %get-tuple-element.55), channel_id=1, source_target_pairs={{0,32},{16,48},{32,0},{48,16},{1,33},{17,49},{33,1},{49,17},{2,34}... | collective-permute-start | bytes 122888 | tf_op jit(solution)/shard_map/ppermute | solution.py:257
  68.8 5.0 %collective-permute-start.10 = (bf16[1,160,128]{2,1,0:T(8,128)(2,1)S(1)}, bf16[1,160,128]{2,1,0:T(8,128)(2,1)S(1)}, u32[]{:S(2)}, u32[]{:S(2)}) collective-permute-start(bf16[1,160,128]{2,1,0:T(8,128)(2,1)S(1)} %get-tuple-element.55), channel_id=1, source_target_pairs={{0,16},{16,0},{32,48},{48,32},{1,17},{17,1},{33,49},{49,33},{2,18}... | collective-permute-start | bytes 122888 | tf_op jit(solution)/shard_map/ppermute | solution.py:257
  74.1 2.9 %collective-permute-start.13 = (bf16[1,160,128]{2,1,0:T(8,128)(2,1)S(1)}, bf16[1,160,128]{2,1,0:T(8,128)(2,1)S(1)}, u32[]{:S(2)}, u32[]{:S(2)}) collective-permute-start(bf16[1,160,128]{2,1,0:T(8,128)(2,1)S(1)} %get-tuple-element.53), channel_id=1, source_target_pairs={{0,64},{4,68},{64,0},{68,4},{128,192},{132,196},{192,128},{196,132... | collective-permute-start | bytes 122888 | tf_op jit(solution)/shard_map/ppermute | solution.py:257
  77.1 6.0 %collective-permute-start.16 = (bf16[1,160,128]{2,1,0:T(8,128)(2,1)S(1)}, bf16[1,160,128]{2,1,0:T(8,128)(2,1)S(1)}, u32[]{:S(2)}, u32[]{:S(2)}) collective-permute-start(bf16[1,160,128]{2,1,0:T(8,128)(2,1)S(1)} %get-tuple-element.51), channel_id=1, source_target_pairs={{0,132},{4,128},{64,196},{68,192},{128,4},{132,0},{192,68},{196,64... | collective-permute-start | bytes 122888 | tf_op jit(solution)/shard_map/ppermute | solution.py:257
  77.2 9.9 %collective-permute-start.15 = (bf16[1,160,128]{2,1,0:T(8,128)(2,1)S(1)}, bf16[1,160,128]{2,1,0:T(8,128)(2,1)S(1)}, u32[]{:S(2)}, u32[]{:S(2)}) collective-permute-start(bf16[1,160,128]{2,1,0:T(8,128)(2,1)S(1)} %get-tuple-element.51), channel_id=1, source_target_pairs={{0,4},{4,0},{64,68},{68,64},{128,132},{132,128},{192,196},{196,192... | collective-permute-start | bytes 122888 | tf_op jit(solution)/shard_map/ppermute | solution.py:257
  83.1 4.0 %collective-permute-start.14 = (bf16[1,160,128]{2,1,0:T(8,128)(2,1)S(1)}, bf16[1,160,128]{2,1,0:T(8,128)(2,1)S(1)}, u32[]{:S(2)}, u32[]{:S(2)}) collective-permute-start(bf16[1,160,128]{2,1,0:T(8,128)(2,1)S(1)} %get-tuple-element.51), channel_id=1, source_target_pairs={{0,128},{4,132},{64,192},{68,196},{128,0},{132,4},{192,64},{196,68... | collective-permute-start | bytes 122888 | tf_op jit(solution)/shard_map/ppermute | solution.py:257
  87.3 3.9 %collective-permute-start.19 = (bf16[1,160,128]{2,1,0:T(8,128)(2,1)S(1)}, bf16[1,160,128]{2,1,0:T(8,128)(2,1)S(1)}, u32[]{:S(2)}, u32[]{:S(2)}) collective-permute-start(bf16[1,160,128]{2,1,0:T(8,128)(2,1)S(1)} %pad_maximum_fusion.11), channel_id=1, source_target_pairs={{0,1},{1,0},{2,3},{3,2},{4,5},{5,4},{6,7},{7,6},{8,9},{9,8},{10,11... | collective-permute-start | bytes 122888 | tf_op jit(solution)/shard_map/ppermute | solution.py:257
  87.9 4.4 %collective-permute-start.18 = (bf16[1,160,128]{2,1,0:T(8,128)(2,1)S(1)}, bf16[1,160,128]{2,1,0:T(8,128)(2,1)S(1)}, u32[]{:S(2)}, u32[]{:S(2)}) collective-permute-start(bf16[1,160,128]{2,1,0:T(8,128)(2,1)S(1)} %pad_maximum_fusion.11), channel_id=1, source_target_pairs={{0,2},{1,3},{2,0},{3,1},{4,6},{5,7},{6,4},{7,5},{8,10},{9,11},{10,... | collective-permute-start | bytes 122888 | tf_op jit(solution)/shard_map/ppermute | solution.py:257
  89.6 4.1 %collective-permute-start.17 = (bf16[1,160,128]{2,1,0:T(8,128)(2,1)S(1)}, bf16[1,160,128]{2,1,0:T(8,128)(2,1)S(1)}, u32[]{:S(2)}, u32[]{:S(2)}) collective-permute-start(bf16[1,160,128]{2,1,0:T(8,128)(2,1)S(1)} %pad_maximum_fusion.11), channel_id=1, source_target_pairs={{0,3},{1,2},{2,1},{3,0},{4,7},{5,6},{6,5},{7,4},{8,11},{9,10},{10,... | collective-permute-start | bytes 122888 | tf_op jit(solution)/shard_map/ppermute | solution.py:257
  93.7 8.2 %collective-permute-start.20 = (bf16[4,160,128]{2,1,0:T(8,128)(2,1)S(1)}, bf16[4,160,128]{2,1,0:T(8,128)(2,1)S(1)}, u32[]{:S(2)}, u32[]{:S(2)}) collective-permute-start(bf16[4,160,128]{2,1,0:T(8,128)(2,1)S(1)} %pad_maximum_fusion.7.mine), channel_id=1, source_target_pairs={{0,8},{8,0},{1,9},{9,1},{2,10},{10,2},{3,11},{11,3},{4,12},{12,4},... | collective-permute-start | bytes 491528 | tf_op jit(solution)/shard_map/ppermute | solution.py:257
where the time goes:
time: 103 us
  starting transfers between devices  41.7 us (40%)
  Pallas kernels  26.4 us (26%)
  waiting for transfers between devices  25.1 us (24%)
  other arithmetic  7.5 us (7%)
  between operations  1.36 us (1%)
    ppermute x15, starting transfers between devices, swapped(): return lax.ppermute(value, axis, [(a, a ^ bit) for a in range(count)])  26 us
    pallas_call x2, Pallas kernels, windows(): pl.pallas_call(functools.partial(window_kernel, steps=steps), grid=(steps...  25.5 us
    ppermute x5, starting transfers between devices, passed_back(): lax.ppermute(value, axes, [(a, (a - 1) % count) for a in range(count)])  15.7 us
    ppermute x15, waiting for transfers between devices, swapped(): return lax.ppermute(value, axis, [(a, a ^ bit) for a in range(count)])  14.7 us
    ppermute x5, waiting for transfers between devices, passed_back(): lax.ppermute(value, axes, [(a, (a - 1) % count) for a in range(count)])  10.4 us
    concatenate x3, other arithmetic, per_device(): both = jnp.concatenate([upstream, tokens], axis=3)  4.7 us
  transfers between devices with their start and end apart: 21, of which 9 were waited for; matrix products, arithmetic and copies ran while one was open for 5% of the time, Pallas kernels for 12%

commit v1 on v0

--- a/solution.py
+++ b/solution.py
@@ -17,8 +17,8 @@
 MAIN = 144
 ROWS = MAIN + 8
 BEGIN_AT = 3
-STEPS_A = 1
-STEPS_B = 2
+STEPS_A = 2
+STEPS_B = 1
 FINISH_AT = 2
 F32 = jnp.float32
 BF16 = jnp.bfloat16

time: 103 us -> 103 us (level)
  starting transfers between devices: 41.7 us -> 43.7 us
  waiting for transfers between devices: 25.1 us -> 23.4 us
    ppermute x15, starting transfers between devices: 26 us -> 28 us  [swapped(): return lax.ppermute(value, axis, [(a, a ^ bit) for a in range(count)])]
    ppermute x5, waiting for transfers between devices: 10.4 us -> 8.99 us  [passed_back(): lax.ppermute(value, axes, [(a, (a - 1) % count) for a in range(count)])]
  transfers between devices with their start and end apart: 21 -> 21, of which waited for: 9 -> 10; matrix products, arithmetic and copies ran while one was open for 5% -> 5% of each run, Pallas kernels for 12% -> 13%
where the time goes in v1:
time: 103 us
  starting transfers between devices  43.7 us (42%)
  Pallas kernels  26.4 us (26%)
  waiting for transfers between devices  23.4 us (23%)
  other arithmetic  7.5 us (7%)
  between operations  1.36 us (1%)
    ppermute x15, starting transfers between devices, swapped(): return lax.ppermute(value, axis, [(a, a ^ bit) for a in range(count)])  28 us
    pallas_call x2, Pallas kernels, windows(): pl.pallas_call(functools.partial(window_kernel, steps=steps), grid=(steps...  25.5 us
    ppermute x5, starting transfers between devices, passed_back(): lax.ppermute(value, axes, [(a, (a - 1) % count) for a in range(count)])  15.7 us
    ppermute x15, waiting for transfers between devices, swapped(): return lax.ppermute(value, axis, [(a, a ^ bit) for a in range(count)])  14.4 us
    ppermute x5, waiting for transfers between devices, passed_back(): lax.ppermute(value, axes, [(a, (a - 1) % count) for a in range(count)])  8.99 us
    concatenate x3, other arithmetic, per_device(): both = jnp.concatenate([upstream, tokens], axis=3)  4.7 us
  transfers between devices with their start and end apart: 21, of which 10 were waited for; matrix products, arithmetic and copies ran while one was open for 5% of the time, Pallas kernels for 13%

profile of v1, /device:TPU:1, one launch (start us, length us, event | category | flops | bytes accessed | tf_op | source)
XLA Modules:
  0.0 103.1 jit_solution(8857305986070133117)
XLA Ops:
  0.6 0.0 copy-start.2
  0.6 0.0 copy-start.3
  0.7 2.1 %fusion.2 = bf16[8,4,16,384]{3,2,1,0:T(8,128)(2,1)} fusion(bf16[8,16,16,192]{3,2,1,0:T(8,128)(2,1)} %param.8, bf16[8,16,16,192]{3,2,1,0:T(8,128)(2,1)} %param.7), kind=kLoop, calls=%fused_computation.15 | loop fusion | flops 786432 | bytes 1966080 | tf_op jit(solution)/shard_map/concatenate | solution.py:380
  2.7 3.2 %collective-permute-start = (bf16[8,4,16,384]{3,2,1,0:T(8,128)(2,1)}, bf16[8,4,16,384]{3,2,1,0:T(8,128)(2,1)S(1)}, u32[]{:S(2)}, u32[]{:S(2)}) collective-permute-start(bf16[8,4,16,384]{3,2,1,0:T(8,128)(2,1)} %fusion.2), channel_id=1, source_target_pairs={{0,8},{8,0},{1,9},{9,1},{2,10},{10,2},{3,11},{11,3},{4,12},{12,4},... | collective-permute-start | bytes 1179656 | tf_op jit(solution)/shard_map/ppermute | solution.py:364
  6.0 0.9 pad_maximum_fusion.3
  6.9 4.8 %collective-permute-start.1 = (bf16[4,12,8,384]{3,2,1,0:T(8,128)(2,1)}, bf16[4,12,8,384]{3,2,1,0:T(8,128)(2,1)S(1)}, u32[]{:S(2)}, u32[]{:S(2)}) collective-permute-start(bf16[4,12,8,384]{3,2,1,0:T(8,128)(2,1)} %pad_maximum_fusion.3), channel_id=1, source_target_pairs={{0,240},{16,0},{32,16},{48,32},{64,48},{80,64},{96,80},{112,96},{1... | collective-permute-start | bytes 884744 | tf_op jit(solution)/shard_map/ppermute | solution.py:364
  11.7 0.1 pad_add_fusion.2.flags
  11.8 1.7 %fusion = bf16[8,12,16,384]{3,2,1,0:T(8,128)(2,1)S(1)} fusion(bf16[8,16,16,192]{3,2,1,0:T(8,128)(2,1)S(1)} %copy-done.2, bf16[8,16,16,192]{3,2,1,0:T(8,128)(2,1)} %param.7), kind=kLoop, calls=%fused_computation.12 | loop fusion | flops 2359296 | bytes 2752512 | tf_op jit(solution)/shard_map/concatenate | solution.py:380
  13.5 0.1 pad_add_fusion.flags
  13.6 0.0 copy-done.5
  13.6 0.1 copy.16.gain
  13.7 0.1 copy.17.nbias
  13.9 0.1 reshape.545.qbias
  14.0 0.2 copy.15
  14.2 0.0 collective-permute-done
  14.2 0.6 collective-permute-start.2
  14.9 0.3 fusion.3
  15.2 0.0 copy-start.1
  15.2 0.3 collective-permute-start.4
  15.6 6.7 %collective-permute-start.3 = (bf16[4,16,4,384]{3,2,1,0:T(4,128)(2,1)S(1)}, bf16[4,16,4,384]{3,2,1,0:T(4,128)(2,1)S(1)}, u32[]{:S(2)}, u32[]{:S(2)}) collective-permute-start(bf16[4,16,4,384]{3,2,1,0:T(4,128)(2,1)S(1)} %get-tuple-element.35), channel_id=1, source_target_pairs={{0,7},{1,0},{2,1},{3,2},{4,3},{5,4},{6,5},{7,6},{8,15},{9,8},{10,9... | collective-permute-start | bytes 589832 | tf_op jit(solution)/shard_map/ppermute | solution.py:364
  22.2 0.0 collective-permute-start.5
  22.2 0.2 fusion.1.near
  22.4 0.0 collective-permute-done.1.rest_0_
  22.4 0.0 collective-permute-done.2.rest_1_
  22.4 13.4 %window_grads.2 = (bf16[8,16,8,192]{3,2,1,0:T(8,128)(2,1)S(1)}, f32[8,152,128]{2,1,0:T(8,128)S(1)}) custom-call(s32[3]{0:T(128)S(1)} %pad_add_fusion.flags, f32[192,1]{1,0:T(8,128)S(1)} %copy.16.gain, f32[192,1]{1,0:T(8,128)S(1)} %copy.17.nbias, bf16[576,192]{1,0:T(8,128)(2,1)S(1)} %bitcast.7, bf16[192,576]{1,0:T(8,128)(2,1)S(1)} %copy-done, ...), custom_call_target="tpu_custom_call" | custom-call | flops 20000000000 | bytes 4000000 | tf_op jit(solution)/shard_map/window_grads/pallas_call | solution.py:225
  35.9 9.0 %collective-permute-done.3 = bf16[4,16,4,384]{3,2,1,0:T(4,128)(2,1)S(1)} collective-permute-done((bf16[4,16,4,384]{3,2,1,0:T(4,128)(2,1)S(1)}, bf16[4,16,4,384]{3,2,1,0:T(4,128)(2,1)S(1)}, u32[]{:S(2)}, u32[]{:S(2)}) %collective-permute-start.3) | collective-permute-done | bytes 196640 | tf_op jit(solution)/shard_map/ppermute | solution.py:364
  44.8 0.2 pad_maximum_fusion.1.near
  45.0 0.0 collective-permute-done.4
  45.1 0.0 collective-permute-done.5
  45.1 0.2 pad_maximum_fusion.2.rest_0_
  45.3 12.1 %window_grads.3 = (bf16[8,16,8,192]{3,2,1,0:T(8,128)(2,1)S(1)}, f32[8,152,128]{2,1,0:T(8,128)S(1)}) custom-call(s32[3]{0:T(128)S(1)} %pad_add_fusion.2.flags, f32[192,1]{1,0:T(8,128)S(1)} %copy.16.gain, f32[192,1]{1,0:T(8,128)S(1)} %copy.17.nbias, bf16[576,192]{1,0:T(8,128)(2,1)S(1)} %bitcast.8, bf16[192,576]{1,0:T(8,128)(2,1)S(1)} %copy-done, ...), custom_call_target="tpu_custom_call" | custom-call | flops 20000000000 | bytes 4000000 | tf_op jit(solution)/shard_map/window_grads/pallas_call | solution.py:225
  57.3 0.1 add.168
  57.5 2.3 %collective-permute-start.6 = (bf16[4,160,128]{2,1,0:T(8,128)(2,1)S(1)}, bf16[4,160,128]{2,1,0:T(8,128)(2,1)S(1)}, u32[]{:S(2)}, u32[]{:S(2)}) collective-permute-start(bf16[4,160,128]{2,1,0:T(8,128)(2,1)S(1)} %pad_maximum_fusion.5), channel_id=1, source_target_pairs={{0,8},{8,0},{1,9},{9,1},{2,10},{10,2},{3,11},{11,3},{4,12},{12,4},... | collective-permute-start | bytes 491528 | tf_op jit(solution)/shard_map/ppermute | solution.py:257
  59.8 1.0 collective-permute-done.6
  61.0 0.1 collective-permute-start.7
  61.1 3.0 %collective-permute-start.9 = (bf16[1,160,128]{2,1,0:T(8,128)(2,1)S(1)}, bf16[1,160,128]{2,1,0:T(8,128)(2,1)S(1)}, u32[]{:S(2)}, u32[]{:S(2)}) collective-permute-start(bf16[1,160,128]{2,1,0:T(8,128)(2,1)S(1)} %get-tuple-element.45), channel_id=1, source_target_pairs={{0,3},{1,2},{2,1},{3,0},{4,7},{5,6},{6,5},{7,4},{8,11},{9,10},{10,... | collective-permute-start | bytes 122888 | tf_op jit(solution)/shard_map/ppermute | solution.py:257
  64.1 0.5 collective-permute-start.8
  64.6 0.9 collective-permute-done.7
  65.5 1.7 %collective-permute-done.8 = bf16[1,160,128]{2,1,0:T(8,128)(2,1)S(1)} collective-permute-done((bf16[1,160,128]{2,1,0:T(8,128)(2,1)S(1)}, bf16[1,160,128]{2,1,0:T(8,128)(2,1)S(1)}, u32[]{:S(2)}, u32[]{:S(2)}) %collective-permute-start.8) | collective-permute-done | bytes 40992 | tf_op jit(solution)/shard_map/ppermute | solution.py:257
  67.3 0.0 collective-permute-done.9
  67.4 0.1 collective-permute-start.12
  67.6 0.1 collective-permute-start.11
  67.7 3.2 %collective-permute-start.10 = (bf16[1,160,128]{2,1,0:T(8,128)(2,1)S(1)}, bf16[1,160,128]{2,1,0:T(8,128)(2,1)S(1)}, u32[]{:S(2)}, u32[]{:S(2)}) collective-permute-start(bf16[1,160,128]{2,1,0:T(8,128)(2,1)S(1)} %get-tuple-element.55), channel_id=1, source_target_pairs={{0,16},{16,0},{32,48},{48,32},{1,17},{17,1},{33,49},{49,33},{2,18}... | collective-permute-start | bytes 122888 | tf_op jit(solution)/shard_map/ppermute | solution.py:257
  70.9 0.7 collective-permute-done.12
  71.6 1.1 %collective-permute-done.10 = bf16[1,160,128]{2,1,0:T(8,128)(2,1)S(1)} collective-permute-done((bf16[1,160,128]{2,1,0:T(8,128)(2,1)S(1)}, bf16[1,160,128]{2,1,0:T(8,128)(2,1)S(1)}, u32[]{:S(2)}, u32[]{:S(2)}) %collective-permute-start.10) | collective-permute-done | bytes 40992 | tf_op jit(solution)/shard_map/ppermute | solution.py:257
  72.7 0.0 collective-permute-done.11
  72.9 0.1 collective-permute-start.13
  73.0 2.8 %collective-permute-done.13 = bf16[1,160,128]{2,1,0:T(8,128)(2,1)S(1)} collective-permute-done((bf16[1,160,128]{2,1,0:T(8,128)(2,1)S(1)}, bf16[1,160,128]{2,1,0:T(8,128)(2,1)S(1)}, u32[]{:S(2)}, u32[]{:S(2)}) %collective-permute-start.13) | collective-permute-done | bytes 40992 | tf_op jit(solution)/shard_map/ppermute | solution.py:257
  76.0 0.1 collective-permute-start.16
  76.1 7.3 %collective-permute-start.15 = (bf16[1,160,128]{2,1,0:T(8,128)(2,1)S(1)}, bf16[1,160,128]{2,1,0:T(8,128)(2,1)S(1)}, u32[]{:S(2)}, u32[]{:S(2)}) collective-permute-start(bf16[1,160,128]{2,1,0:T(8,128)(2,1)S(1)} %get-tuple-element.51), channel_id=1, source_target_pairs={{0,4},{4,0},{64,68},{68,64},{128,132},{132,128},{192,196},{196,192... | collective-permute-start | bytes 122888 | tf_op jit(solution)/shard_map/ppermute | solution.py:257
  83.3 0.0 collective-permute-start.14
  83.3 0.0 collective-permute-done.16
  83.4 3.7 %collective-permute-done.14 = bf16[1,160,128]{2,1,0:T(8,128)(2,1)S(1)} collective-permute-done((bf16[1,160,128]{2,1,0:T(8,128)(2,1)S(1)}, bf16[1,160,128]{2,1,0:T(8,128)(2,1)S(1)}, u32[]{:S(2)}, u32[]{:S(2)}) %collective-permute-start.14) | collective-permute-done | bytes 40992 | tf_op jit(solution)/shard_map/ppermute | solution.py:257
  87.1 0.0 collective-permute-done.15
  87.3 0.7 collective-permute-start.19
  88.0 1.6 %collective-permute-start.18 = (bf16[1,160,128]{2,1,0:T(8,128)(2,1)S(1)}, bf16[1,160,128]{2,1,0:T(8,128)(2,1)S(1)}, u32[]{:S(2)}, u32[]{:S(2)}) collective-permute-start(bf16[1,160,128]{2,1,0:T(8,128)(2,1)S(1)} %pad_maximum_fusion.11), channel_id=1, source_target_pairs={{0,2},{1,3},{2,0},{3,1},{4,6},{5,7},{6,4},{7,5},{8,10},{9,11},{10,... | collective-permute-start | bytes 122888 | tf_op jit(solution)/shard_map/ppermute | solution.py:257
  89.5 1.7 %collective-permute-start.17 = (bf16[1,160,128]{2,1,0:T(8,128)(2,1)S(1)}, bf16[1,160,128]{2,1,0:T(8,128)(2,1)S(1)}, u32[]{:S(2)}, u32[]{:S(2)}) collective-permute-start(bf16[1,160,128]{2,1,0:T(8,128)(2,1)S(1)} %pad_maximum_fusion.11), channel_id=1, source_target_pairs={{0,3},{1,2},{2,1},{3,0},{4,7},{5,6},{6,5},{7,4},{8,11},{9,10},{10,... | collective-permute-start | bytes 122888 | tf_op jit(solution)/shard_map/ppermute | solution.py:257
  91.2 0.0 collective-permute-done.19
  91.2 1.1 %collective-permute-done.18 = bf16[1,160,128]{2,1,0:T(8,128)(2,1)S(1)} collective-permute-done((bf16[1,160,128]{2,1,0:T(8,128)(2,1)S(1)}, bf16[1,160,128]{2,1,0:T(8,128)(2,1)S(1)}, u32[]{:S(2)}, u32[]{:S(2)}) %collective-permute-start.18) | collective-permute-done | bytes 40992 | tf_op jit(solution)/shard_map/ppermute | solution.py:257
  92.3 1.3 %collective-permute-done.17 = bf16[1,160,128]{2,1,0:T(8,128)(2,1)S(1)} collective-permute-done((bf16[1,160,128]{2,1,0:T(8,128)(2,1)S(1)}, bf16[1,160,128]{2,1,0:T(8,128)(2,1)S(1)}, u32[]{:S(2)}, u32[]{:S(2)}) %collective-permute-start.17) | collective-permute-done | bytes 40992 | tf_op jit(solution)/shard_map/ppermute | solution.py:257
  93.7 7.3 %collective-permute-start.20 = (bf16[4,160,128]{2,1,0:T(8,128)(2,1)S(1)}, bf16[4,160,128]{2,1,0:T(8,128)(2,1)S(1)}, u32[]{:S(2)}, u32[]{:S(2)}) collective-permute-start(bf16[4,160,128]{2,1,0:T(8,128)(2,1)S(1)} %pad_maximum_fusion.7.mine), channel_id=1, source_target_pairs={{0,8},{8,0},{1,9},{9,1},{2,10},{10,2},{3,11},{11,3},{4,12},{12,4},... | collective-permute-start | bytes 491528 | tf_op jit(solution)/shard_map/ppermute | solution.py:257
  101.0 1.2 %pad_maximum_fusion = bf16[8,16,16,192]{3,2,1,0:T(8,128)(2,1)} fusion(bf16[8,16,8,192]{3,2,1,0:T(8,128)(2,1)S(1)} %get-tuple-element.18, bf16[8,16,8,192]{3,2,1,0:T(8,128)(2,1)S(1)} %get-tuple-element.17), kind=kLoop, calls=%fused_computation.13 | loop fusion | flops 1572864 | bytes 1572864 | tf_op jit(solution)/shard_map/concatenate | solution.py:417
  102.2 0.0 collective-permute-done.20.other
  102.2 0.9 unpack_sums.1
  (79 shorter events, 0.8 us)
Async XLA Ops:
  0.6 5.3 %copy-start.2 = (bf16[8,16,16,192]{3,2,1,0:T(8,128)(2,1)S(1)}, bf16[8,16,16,192]{3,2,1,0:T(8,128)(2,1)}, u32[]{:S(2)}) copy-start(bf16[8,16,16,192]{3,2,1,0:T(8,128)(2,1)} %param.8) | copy-start | bytes 2359300
  0.6 5.3 %copy-start.3 = (bf16[8,16,16,192]{3,2,1,0:T(8,128)(2,1)S(1)}, bf16[8,16,16,192]{3,2,1,0:T(8,128)(2,1)}, u32[]{:S(2)}) copy-start(bf16[8,16,16,192]{3,2,1,0:T(8,128)(2,1)} %param.7) | copy-start | bytes 2359300
  2.7 11.4 %collective-permute-start = (bf16[8,4,16,384]{3,2,1,0:T(8,128)(2,1)}, bf16[8,4,16,384]{3,2,1,0:T(8,128)(2,1)S(1)}, u32[]{:S(2)}, u32[]{:S(2)}) collective-permute-start(bf16[8,4,16,384]{3,2,1,0:T(8,128)(2,1)} %fusion.2), channel_id=1, source_target_pairs={{0,8},{8,0},{1,9},{9,1},{2,10},{10,2},{3,11},{11,3},{4,12},{12,4},... | collective-permute-start | bytes 1179656 | tf_op jit(solution)/shard_map/ppermute | solution.py:364
  6.9 15.5 %collective-permute-start.1 = (bf16[4,12,8,384]{3,2,1,0:T(8,128)(2,1)}, bf16[4,12,8,384]{3,2,1,0:T(8,128)(2,1)S(1)}, u32[]{:S(2)}, u32[]{:S(2)}) collective-permute-start(bf16[4,12,8,384]{3,2,1,0:T(8,128)(2,1)} %pad_maximum_fusion.3), channel_id=1, source_target_pairs={{0,240},{16,0},{32,16},{48,32},{64,48},{80,64},{96,80},{112,96},{1... | collective-permute-start | bytes 884744 | tf_op jit(solution)/shard_map/ppermute | solution.py:364
  11.8 1.8 %copy-start.5 = (f32[192]{0:T(256)S(1)}, f32[192]{0:T(256)}, u32[]{:S(2)}) copy-start(f32[192]{0:T(256)} %param.9) | copy-start | bytes 2308
  11.8 1.9 %copy-start.6 = (f32[192]{0:T(256)S(1)}, f32[192]{0:T(256)}, u32[]{:S(2)}) copy-start(f32[192]{0:T(256)} %param.10) | copy-start | bytes 2308
  11.8 2.1 %copy-start.4 = (f32[576]{0:T(1024)S(1)}, f32[576]{0:T(1024)}, u32[]{:S(2)}) copy-start(f32[576]{0:T(1024)} %param.12) | copy-start | bytes 6916
  11.8 2.2 %copy-start = (bf16[192,576]{1,0:T(8,128)(2,1)S(1)}, bf16[192,576]{1,0:T(8,128)(2,1)}, u32[]{:S(2)}) copy-start(bf16[192,576]{1,0:T(8,128)(2,1)} %w_rows.3) | copy-start | bytes 663556
  14.2 8.2 %collective-permute-start.2 = (bf16[4,4,8,384]{3,2,1,0:T(8,128)(2,1)S(1)}, bf16[4,4,8,384]{3,2,1,0:T(8,128)(2,1)S(1)}, u32[]{:S(2)}, u32[]{:S(2)}) collective-permute-start(bf16[4,4,8,384]{3,2,1,0:T(8,128)(2,1)S(1)} %slice.264), channel_id=1, source_target_pairs={{0,240},{16,0},{32,16},{48,32},{64,48},{80,64},{96,80},{112,96},{1... | collective-permute-start | bytes 294920 | tf_op jit(solution)/shard_map/ppermute | solution.py:364
  15.2 7.2 %copy-start.1 = (bf16[192,192]{1,0:T(8,128)(2,1)S(1)}, bf16[192,192]{1,0:T(8,128)(2,1)}, u32[]{:S(2)}) copy-start(bf16[192,192]{1,0:T(8,128)(2,1)} %proj.3) | copy-start | bytes 221188
  15.2 29.8 %collective-permute-start.4 = (bf16[4,16,4,384]{3,2,1,0:T(4,128)(2,1)S(1)}, bf16[4,16,4,384]{3,2,1,0:T(4,128)(2,1)S(1)}, u32[]{:S(2)}, u32[]{:S(2)}) collective-permute-start(bf16[4,16,4,384]{3,2,1,0:T(4,128)(2,1)S(1)} %get-tuple-element.33), channel_id=1, source_target_pairs={{0,240},{16,0},{32,16},{48,32},{64,48},{80,64},{96,80},{112,96},{1... | collective-permute-start | bytes 589832 | tf_op jit(solution)/shard_map/ppermute | solution.py:364
  15.6 29.3 %collective-permute-start.3 = (bf16[4,16,4,384]{3,2,1,0:T(4,128)(2,1)S(1)}, bf16[4,16,4,384]{3,2,1,0:T(4,128)(2,1)S(1)}, u32[]{:S(2)}, u32[]{:S(2)}) collective-permute-start(bf16[4,16,4,384]{3,2,1,0:T(4,128)(2,1)S(1)} %get-tuple-element.35), channel_id=1, source_target_pairs={{0,7},{1,0},{2,1},{3,2},{4,3},{5,4},{6,5},{7,6},{8,15},{9,8},{10,9... | collective-permute-start | bytes 589832 | tf_op jit(solution)/shard_map/ppermute | solution.py:364
  22.2 22.8 %collective-permute-start.5 = (bf16[4,16,4,384]{3,2,1,0:T(4,128)(2,1)S(1)}, bf16[4,16,4,384]{3,2,1,0:T(4,128)(2,1)S(1)}, u32[]{:S(2)}, u32[]{:S(2)}) collective-permute-start(bf16[4,16,4,384]{3,2,1,0:T(4,128)(2,1)S(1)} %get-tuple-element.36), channel_id=1, source_target_pairs={{0,247},{1,240},{2,241},{3,242},{4,243},{5,244},{6,245},{7,246},{1... | collective-permute-start | bytes 589832 | tf_op jit(solution)/shard_map/ppermute | solution.py:374
  57.5 3.3 %collective-permute-start.6 = (bf16[4,160,128]{2,1,0:T(8,128)(2,1)S(1)}, bf16[4,160,128]{2,1,0:T(8,128)(2,1)S(1)}, u32[]{:S(2)}, u32[]{:S(2)}) collective-permute-start(bf16[4,160,128]{2,1,0:T(8,128)(2,1)S(1)} %pad_maximum_fusion.5), channel_id=1, source_target_pairs={{0,8},{8,0},{1,9},{9,1},{2,10},{10,2},{3,11},{11,3},{4,12},{12,4},... | collective-permute-start | bytes 491528 | tf_op jit(solution)/shard_map/ppermute | solution.py:257
  61.0 4.5 %collective-permute-start.7 = (bf16[1,160,128]{2,1,0:T(8,128)(2,1)S(1)}, bf16[1,160,128]{2,1,0:T(8,128)(2,1)S(1)}, u32[]{:S(2)}, u32[]{:S(2)}) collective-permute-start(bf16[1,160,128]{2,1,0:T(8,128)(2,1)S(1)} %get-tuple-element.47), channel_id=1, source_target_pairs={{0,2},{1,3},{2,0},{3,1},{4,6},{5,7},{6,4},{7,5},{8,10},{9,11},{10,... | collective-permute-start | bytes 122888 | tf_op jit(solution)/shard_map/ppermute | solution.py:257
  61.1 6.1 %collective-permute-start.9 = (bf16[1,160,128]{2,1,0:T(8,128)(2,1)S(1)}, bf16[1,160,128]{2,1,0:T(8,128)(2,1)S(1)}, u32[]{:S(2)}, u32[]{:S(2)}) collective-permute-start(bf16[1,160,128]{2,1,0:T(8,128)(2,1)S(1)} %get-tuple-element.45), channel_id=1, source_target_pairs={{0,3},{1,2},{2,1},{3,0},{4,7},{5,6},{6,5},{7,4},{8,11},{9,10},{10,... | collective-permute-start | bytes 122888 | tf_op jit(solution)/shard_map/ppermute | solution.py:257
  64.1 3.1 %collective-permute-start.8 = (bf16[1,160,128]{2,1,0:T(8,128)(2,1)S(1)}, bf16[1,160,128]{2,1,0:T(8,128)(2,1)S(1)}, u32[]{:S(2)}, u32[]{:S(2)}) collective-permute-start(bf16[1,160,128]{2,1,0:T(8,128)(2,1)S(1)} %get-tuple-element.46), channel_id=1, source_target_pairs={{0,1},{1,0},{2,3},{3,2},{4,5},{5,4},{6,7},{7,6},{8,9},{9,8},{10,11... | collective-permute-start | bytes 122888 | tf_op jit(solution)/shard_map/ppermute | solution.py:257
  67.4 4.2 %collective-permute-start.12 = (bf16[1,160,128]{2,1,0:T(8,128)(2,1)S(1)}, bf16[1,160,128]{2,1,0:T(8,128)(2,1)S(1)}, u32[]{:S(2)}, u32[]{:S(2)}) collective-permute-start(bf16[1,160,128]{2,1,0:T(8,128)(2,1)S(1)} %get-tuple-element.55), channel_id=1, source_target_pairs={{0,48},{16,32},{32,16},{48,0},{1,49},{17,33},{33,17},{49,1},{2,50}... | collective-permute-start | bytes 122888 | tf_op jit(solution)/shard_map/ppermute | solution.py:257
  67.6 5.2 %collective-permute-start.11 = (bf16[1,160,128]{2,1,0:T(8,128)(2,1)S(1)}, bf16[1,160,128]{2,1,0:T(8,128)(2,1)S(1)}, u32[]{:S(2)}, u32[]{:S(2)}) collective-permute-start(bf16[1,160,128]{2,1,0:T(8,128)(2,1)S(1)} %get-tuple-element.55), channel_id=1, source_target_pairs={{0,32},{16,48},{32,0},{48,16},{1,33},{17,49},{33,1},{49,17},{2,34}... | collective-permute-start | bytes 122888 | tf_op jit(solution)/shard_map/ppermute | solution.py:257
  67.7 5.0 %collective-permute-start.10 = (bf16[1,160,128]{2,1,0:T(8,128)(2,1)S(1)}, bf16[1,160,128]{2,1,0:T(8,128)(2,1)S(1)}, u32[]{:S(2)}, u32[]{:S(2)}) collective-permute-start(bf16[1,160,128]{2,1,0:T(8,128)(2,1)S(1)} %get-tuple-element.55), channel_id=1, source_target_pairs={{0,16},{16,0},{32,48},{48,32},{1,17},{17,1},{33,49},{49,33},{2,18}... | collective-permute-start | bytes 122888 | tf_op jit(solution)/shard_map/ppermute | solution.py:257
  72.9 2.9 %collective-permute-start.13 = (bf16[1,160,128]{2,1,0:T(8,128)(2,1)S(1)}, bf16[1,160,128]{2,1,0:T(8,128)(2,1)S(1)}, u32[]{:S(2)}, u32[]{:S(2)}) collective-permute-start(bf16[1,160,128]{2,1,0:T(8,128)(2,1)S(1)} %get-tuple-element.53), channel_id=1, source_target_pairs={{0,64},{4,68},{64,0},{68,4},{128,192},{132,196},{192,128},{196,132... | collective-permute-start | bytes 122888 | tf_op jit(solution)/shard_map/ppermute | solution.py:257
  76.0 7.4 %collective-permute-start.16 = (bf16[1,160,128]{2,1,0:T(8,128)(2,1)S(1)}, bf16[1,160,128]{2,1,0:T(8,128)(2,1)S(1)}, u32[]{:S(2)}, u32[]{:S(2)}) collective-permute-start(bf16[1,160,128]{2,1,0:T(8,128)(2,1)S(1)} %get-tuple-element.51), channel_id=1, source_target_pairs={{0,132},{4,128},{64,196},{68,192},{128,4},{132,0},{192,68},{196,64... | collective-permute-start | bytes 122888 | tf_op jit(solution)/shard_map/ppermute | solution.py:257
  76.1 11.0 %collective-permute-start.15 = (bf16[1,160,128]{2,1,0:T(8,128)(2,1)S(1)}, bf16[1,160,128]{2,1,0:T(8,128)(2,1)S(1)}, u32[]{:S(2)}, u32[]{:S(2)}) collective-permute-start(bf16[1,160,128]{2,1,0:T(8,128)(2,1)S(1)} %get-tuple-element.51), channel_id=1, source_target_pairs={{0,4},{4,0},{64,68},{68,64},{128,132},{132,128},{192,196},{196,192... | collective-permute-start | bytes 122888 | tf_op jit(solution)/shard_map/ppermute | solution.py:257
  83.3 3.8 %collective-permute-start.14 = (bf16[1,160,128]{2,1,0:T(8,128)(2,1)S(1)}, bf16[1,160,128]{2,1,0:T(8,128)(2,1)S(1)}, u32[]{:S(2)}, u32[]{:S(2)}) collective-permute-start(bf16[1,160,128]{2,1,0:T(8,128)(2,1)S(1)} %get-tuple-element.51), channel_id=1, source_target_pairs={{0,128},{4,132},{64,192},{68,196},{128,0},{132,4},{192,64},{196,68... | collective-permute-start | bytes 122888 | tf_op jit(solution)/shard_map/ppermute | solution.py:257
  87.3 3.9 %collective-permute-start.19 = (bf16[1,160,128]{2,1,0:T(8,128)(2,1)S(1)}, bf16[1,160,128]{2,1,0:T(8,128)(2,1)S(1)}, u32[]{:S(2)}, u32[]{:S(2)}) collective-permute-start(bf16[1,160,128]{2,1,0:T(8,128)(2,1)S(1)} %pad_maximum_fusion.11), channel_id=1, source_target_pairs={{0,1},{1,0},{2,3},{3,2},{4,5},{5,4},{6,7},{7,6},{8,9},{9,8},{10,11... | collective-permute-start | bytes 122888 | tf_op jit(solution)/shard_map/ppermute | solution.py:257
  88.0 4.4 %collective-permute-start.18 = (bf16[1,160,128]{2,1,0:T(8,128)(2,1)S(1)}, bf16[1,160,128]{2,1,0:T(8,128)(2,1)S(1)}, u32[]{:S(2)}, u32[]{:S(2)}) collective-permute-start(bf16[1,160,128]{2,1,0:T(8,128)(2,1)S(1)} %pad_maximum_fusion.11), channel_id=1, source_target_pairs={{0,2},{1,3},{2,0},{3,1},{4,6},{5,7},{6,4},{7,5},{8,10},{9,11},{10,... | collective-permute-start | bytes 122888 | tf_op jit(solution)/shard_map/ppermute | solution.py:257
  89.5 4.1 %collective-permute-start.17 = (bf16[1,160,128]{2,1,0:T(8,128)(2,1)S(1)}, bf16[1,160,128]{2,1,0:T(8,128)(2,1)S(1)}, u32[]{:S(2)}, u32[]{:S(2)}) collective-permute-start(bf16[1,160,128]{2,1,0:T(8,128)(2,1)S(1)} %pad_maximum_fusion.11), channel_id=1, source_target_pairs={{0,3},{1,2},{2,1},{3,0},{4,7},{5,6},{6,5},{7,4},{8,11},{9,10},{10,... | collective-permute-start | bytes 122888 | tf_op jit(solution)/shard_map/ppermute | solution.py:257
  93.7 8.5 %collective-permute-start.20 = (bf16[4,160,128]{2,1,0:T(8,128)(2,1)S(1)}, bf16[4,160,128]{2,1,0:T(8,128)(2,1)S(1)}, u32[]{:S(2)}, u32[]{:S(2)}) collective-permute-start(bf16[4,160,128]{2,1,0:T(8,128)(2,1)S(1)} %pad_maximum_fusion.7.mine), channel_id=1, source_target_pairs={{0,8},{8,0},{1,9},{9,1},{2,10},{10,2},{3,11},{11,3},{4,12},{12,4},... | collective-permute-start | bytes 491528 | tf_op jit(solution)/shard_map/ppermute | solution.py:257

commit v2 on v0

--- a/solution.py
+++ b/solution.py
@@ -259,14 +259,13 @@
 
 def coded(value):
     small = value[:, MAIN:]
-    high = lax.reduce_precision(small, 8, 7)
-    return jnp.concatenate([value[:, :MAIN], high, small - high], axis=1).astype(BF16)
+    low = small - lax.reduce_precision(small, 8, 7)
+    return jnp.concatenate([value, low], axis=1).astype(BF16)
 
 
 def decoded(value):
     wide = value.astype(F32)
-    small = wide[:, MAIN:ROWS] + wide[:, ROWS:]
-    return jnp.concatenate([wide[:, :MAIN], small], axis=1)
+    return wide[:, :ROWS] + jnp.pad(wide[:, ROWS:], ((0, 0), (MAIN, 0), (0, 0)))
 
 
 def halve(value, axis):
@@ -321,10 +320,16 @@
     return join_four(coded(value), "y")
 
 
+def opened(value):
+    wide = value.astype(F32)
+    small = wide[:, MAIN:ROWS] + wide[:, ROWS:]
+    return jnp.concatenate([wide[:, :MAIN], small], axis=1)
+
+
 def unpack_kernel(upper, mine, other, qkv, proj, qbias, pbias, gain, nbias, *, width, factor):
     here = upper[0] == 1
-    first = decoded(jnp.where(here, other[...], mine[...])) * factor
-    second = decoded(jnp.where(here, mine[...], other[...])) * factor
+    first = opened(jnp.where(here, other[...], mine[...])) * factor
+    second = opened(jnp.where(here, mine[...], other[...])) * factor
     both = jnp.concatenate([first, second], axis=0)
     main = both[:, :MAIN].reshape(PARTS * MAIN, LANES)
     block = lambda j: main[width * j : width * (j + 1)]

time: 103 us -> 106 us (1.029)
  starting transfers between devices: 41.7 us -> 47.5 us
  waiting for transfers between devices: 25.1 us -> 19.5 us
  other arithmetic: 7.5 us -> 9.4 us
    ppermute x5, waiting for transfers between devices: 10.4 us -> 3.57 us  [passed_back(): lax.ppermute(value, axes, [(a, (a - 1) % count) for a in range(count)])]
    ppermute x15, starting transfers between devices: 26 us -> 31.8 us  [swapped(): return lax.ppermute(value, axis, [(a, a ^ bit) for a in range(count)])]
    concatenate x2, other arithmetic: 0.5 us -> 2.45 us  [per_device(): both = jnp.concatenate([both[:, SHIFT:], came_y], axis=1)]
    ppermute x15, waiting for transfers between devices: 14.7 us -> 15.9 us  [swapped(): return lax.ppermute(value, axis, [(a, a ^ bit) for a in range(count)])]
  transfers between devices with their start and end apart: 21 -> 21, of which waited for: 9 -> 12; matrix products, arithmetic and copies ran while one was open for 5% -> 8% of each run, Pallas kernels for 12% -> 11%
where the time goes in v2:
time: 106 us; the launch traced here: 105 us
  starting transfers between devices  47.5 us (45%)
  Pallas kernels  26.4 us (25%)
  waiting for transfers between devices  19.5 us (18%)
  other arithmetic  9.4 us (9%)
  local copies, waits for them, and re-layouts  1.59 us (2%)
  between operations  1.06 us (1%)
    ppermute x15, starting transfers between devices, swapped(): return lax.ppermute(value, axis, [(a, a ^ bit) for a in range(count)])  31.8 us
    pallas_call x2, Pallas kernels, windows(): pl.pallas_call(functools.partial(window_kernel, steps=steps), grid=(steps...  25.5 us
    ppermute x15, waiting for transfers between devices, swapped(): return lax.ppermute(value, axis, [(a, a ^ bit) for a in range(count)])  15.9 us
    ppermute x5, starting transfers between devices, passed_back(): lax.ppermute(value, axes, [(a, (a - 1) % count) for a in range(count)])  15.7 us
    concatenate x3, other arithmetic, per_device(): both = jnp.concatenate([upstream, tokens], axis=3)  4.7 us
    ppermute x5, waiting for transfers between devices, passed_back(): lax.ppermute(value, axes, [(a, (a - 1) % count) for a in range(count)])  3.57 us
    concatenate x2, other arithmetic, per_device(): both = jnp.concatenate([both[:, SHIFT:], came_y], axis=1)  2.45 us
  transfers between devices with their start and end apart: 21, of which 12 were waited for; matrix products, arithmetic and copies ran while one was open for 8% of the time, Pallas kernels for 11%

profile of v2, /device:TPU:1, one launch (start us, length us, event | category | flops | bytes accessed | tf_op | source)
XLA Modules:
  0.0 105.4 jit_solution(16592444219057318937)
XLA Ops:
  0.6 0.0 copy-start.3
  0.7 2.1 %fusion.2 = bf16[8,4,16,384]{3,2,1,0:T(8,128)(2,1)} fusion(bf16[8,16,16,192]{3,2,1,0:T(8,128)(2,1)} %param.8, bf16[8,16,16,192]{3,2,1,0:T(8,128)(2,1)} %param.7), kind=kLoop, calls=%fused_computation.15 | loop fusion | flops 786432 | bytes 1966080 | tf_op jit(solution)/shard_map/concatenate | solution.py:385
  2.7 3.2 %collective-permute-start = (bf16[8,4,16,384]{3,2,1,0:T(8,128)(2,1)}, bf16[8,4,16,384]{3,2,1,0:T(8,128)(2,1)}, u32[]{:S(2)}, u32[]{:S(2)}) collective-permute-start(bf16[8,4,16,384]{3,2,1,0:T(8,128)(2,1)} %fusion.2), channel_id=1, source_target_pairs={{0,8},{8,0},{1,9},{9,1},{2,10},{10,2},{3,11},{11,3},{4,12},{12,4},... | collective-permute-start | bytes 1179656 | tf_op jit(solution)/shard_map/ppermute | solution.py:369
  6.0 0.9 pad_maximum_fusion.3
  6.9 4.8 %collective-permute-start.1 = (bf16[4,12,8,384]{3,2,1,0:T(8,128)(2,1)}, bf16[4,12,8,384]{3,2,1,0:T(8,128)(2,1)S(1)}, u32[]{:S(2)}, u32[]{:S(2)}) collective-permute-start(bf16[4,12,8,384]{3,2,1,0:T(8,128)(2,1)} %pad_maximum_fusion.3), channel_id=1, source_target_pairs={{0,240},{16,0},{32,16},{48,32},{64,48},{80,64},{96,80},{112,96},{1... | collective-permute-start | bytes 884744 | tf_op jit(solution)/shard_map/ppermute | solution.py:369
  11.7 0.1 pad_add_fusion.2.flags
  11.8 1.7 %fusion = bf16[8,12,16,384]{3,2,1,0:T(8,128)(2,1)S(1)} fusion(bf16[8,16,16,192]{3,2,1,0:T(8,128)(2,1)S(1)} %copy-done.2, bf16[8,16,16,192]{3,2,1,0:T(8,128)(2,1)} %param.7), kind=kLoop, calls=%fused_computation.12 | loop fusion | flops 2359296 | bytes 2752512 | tf_op jit(solution)/shard_map/concatenate | solution.py:385
  13.5 0.1 pad_add_fusion.flags
  13.6 0.1 copy.16.gain
  13.7 0.1 copy.17.nbias
  13.9 0.1 reshape.205.qbias
  14.0 0.2 copy.15
  14.2 0.0 collective-permute-done
  14.2 1.0 slice.178
  15.2 0.6 collective-permute-start.2
  15.8 1.4 %fusion.4 = (bf16[4,16,4,384]{3,2,1,0:T(4,128)(2,1)S(1)}, bf16[4,16,4,384]{3,2,1,0:T(4,128)(2,1)S(1)}, bf16[4,16,4,384]{3,2,1,0:T(4,128)(2,1)S(1)}, bf16[4,16,4,384]{3,2,1,0:T(4,128)(2,1)S(1)}) fusion(bf16[8,12,16,384]{3,2,1,0:T(8,128)(2,1)S(1)} %fusion, bf16[8,4,16,384]{3,2,1,0:T(8,128)(2,1)} %collective-permute-done), kind=kLoop, calls=%fused_computation.25 | loop fusion | flops 1572864 | bytes 2359296 | tf_op jit(solution)/shard_map/concatenate | solution.py:390
  17.2 0.0 copy-start.1
  17.2 0.3 collective-permute-start.4
  17.5 6.7 %collective-permute-start.3 = (bf16[4,16,4,384]{3,2,1,0:T(4,128)(2,1)S(1)}, bf16[4,16,4,384]{3,2,1,0:T(4,128)(2,1)S(1)}, u32[]{:S(2)}, u32[]{:S(2)}) collective-permute-start(bf16[4,16,4,384]{3,2,1,0:T(4,128)(2,1)S(1)} %get-tuple-element.39), channel_id=1, source_target_pairs={{0,7},{1,0},{2,1},{3,2},{4,3},{5,4},{6,5},{7,6},{8,15},{9,8},{10,9... | collective-permute-start | bytes 589832 | tf_op jit(solution)/shard_map/ppermute | solution.py:369
  24.2 0.0 collective-permute-start.5
  24.2 1.1 %fusion.1.near = bf16[4,16,8,384]{3,2,1,0:T(8,128)(2,1)S(1)} fusion(bf16[8,12,16,384]{3,2,1,0:T(8,128)(2,1)S(1)} %fusion, bf16[8,4,16,384]{3,2,1,0:T(8,128)(2,1)} %collective-permute-done), kind=kLoop, calls=%fused_computation.14 | loop fusion | flops 196608 | bytes 1966080 | tf_op jit(solution)/shard_map/concatenate | solution.py:390
  25.3 0.0 collective-permute-done.1.rest_0_
  25.3 0.0 collective-permute-done.2.rest_1_
  25.3 12.0 %window_grads.2 = (bf16[8,16,8,192]{3,2,1,0:T(8,128)(2,1)S(1)}, f32[8,152,128]{2,1,0:T(8,128)S(1)}) custom-call(s32[3]{0:T(128)S(1)} %pad_add_fusion.flags, f32[192,1]{1,0:T(8,128)S(1)} %copy.16.gain, f32[192,1]{1,0:T(8,128)S(1)} %copy.17.nbias, bf16[576,192]{1,0:T(8,128)(2,1)S(1)} %bitcast.7, bf16[192,576]{1,0:T(8,128)(2,1)S(1)} %copy-done, ...), custom_call_target="tpu_custom_call" | custom-call | flops 20000000000 | bytes 4000000 | tf_op jit(solution)/shard_map/window_grads/pallas_call | solution.py:225
  37.3 3.6 %collective-permute-done.3 = bf16[4,16,4,384]{3,2,1,0:T(4,128)(2,1)S(1)} collective-permute-done((bf16[4,16,4,384]{3,2,1,0:T(4,128)(2,1)S(1)}, bf16[4,16,4,384]{3,2,1,0:T(4,128)(2,1)S(1)}, u32[]{:S(2)}, u32[]{:S(2)}) %collective-permute-start.3) | collective-permute-done | bytes 196640 | tf_op jit(solution)/shard_map/ppermute | solution.py:369
  40.9 0.2 pad_maximum_fusion.1.near
  41.1 0.0 collective-permute-done.4
  41.1 0.0 collective-permute-done.5
  41.1 0.2 pad_maximum_fusion.2.rest_0_
  41.3 13.4 %window_grads.3 = (bf16[8,16,8,192]{3,2,1,0:T(8,128)(2,1)S(1)}, f32[8,152,128]{2,1,0:T(8,128)S(1)}) custom-call(s32[3]{0:T(128)S(1)} %pad_add_fusion.2.flags, f32[192,1]{1,0:T(8,128)S(1)} %copy.16.gain, f32[192,1]{1,0:T(8,128)S(1)} %copy.17.nbias, bf16[576,192]{1,0:T(8,128)(2,1)S(1)} %bitcast.8, bf16[192,576]{1,0:T(8,128)(2,1)S(1)} %copy-done, ...), custom_call_target="tpu_custom_call" | custom-call | flops 20000000000 | bytes 4000000 | tf_op jit(solution)/shard_map/window_grads/pallas_call | solution.py:225
  54.8 0.1 add.140
  54.9 1.0 collective-permute-start.6
  56.0 1.0 collective-permute-done.6
  57.0 0.1 fusion.37
  57.1 0.1 collective-permute-start.7
  57.2 8.6 %collective-permute-start.8 = (bf16[1,160,128]{2,1,0:T(8,128)(2,1)S(1)}, bf16[1,160,128]{2,1,0:T(8,128)(2,1)S(1)}, u32[]{:S(2)}, u32[]{:S(2)}) collective-permute-start(bf16[1,160,128]{2,1,0:T(8,128)(2,1)S(1)} %get-tuple-element.46), channel_id=1, source_target_pairs={{0,1},{1,0},{2,3},{3,2},{4,5},{5,4},{6,7},{7,6},{8,9},{9,8},{10,11... | collective-permute-start | bytes 122888 | tf_op jit(solution)/shard_map/ppermute | solution.py:257
  65.8 0.0 collective-permute-start.9
  65.8 0.0 collective-permute-done.7
  65.8 1.9 %collective-permute-done.8 = bf16[1,160,128]{2,1,0:T(8,128)(2,1)S(1)} collective-permute-done((bf16[1,160,128]{2,1,0:T(8,128)(2,1)S(1)}, bf16[1,160,128]{2,1,0:T(8,128)(2,1)S(1)}, u32[]{:S(2)}, u32[]{:S(2)}) %collective-permute-start.8) | collective-permute-done | bytes 40992 | tf_op jit(solution)/shard_map/ppermute | solution.py:257
  67.7 2.1 %collective-permute-done.9 = bf16[1,160,128]{2,1,0:T(8,128)(2,1)S(1)} collective-permute-done((bf16[1,160,128]{2,1,0:T(8,128)(2,1)S(1)}, bf16[1,160,128]{2,1,0:T(8,128)(2,1)S(1)}, u32[]{:S(2)}, u32[]{:S(2)}) %collective-permute-start.9) | collective-permute-done | bytes 40992 | tf_op jit(solution)/shard_map/ppermute | solution.py:257
  69.9 0.1 collective-permute-start.11
  70.0 2.6 %collective-permute-start.10 = (bf16[1,160,128]{2,1,0:T(8,128)(2,1)S(1)}, bf16[1,160,128]{2,1,0:T(8,128)(2,1)S(1)}, u32[]{:S(2)}, u32[]{:S(2)}) collective-permute-start(bf16[1,160,128]{2,1,0:T(8,128)(2,1)S(1)} %get-tuple-element.53), channel_id=1, source_target_pairs={{0,16},{16,0},{32,48},{48,32},{1,17},{17,1},{33,49},{49,33},{2,18}... | collective-permute-start | bytes 122888 | tf_op jit(solution)/shard_map/ppermute | solution.py:257
  72.7 0.6 collective-permute-start.12
  73.3 1.1 %collective-permute-done.11 = bf16[1,160,128]{2,1,0:T(8,128)(2,1)S(1)} collective-permute-done((bf16[1,160,128]{2,1,0:T(8,128)(2,1)S(1)}, bf16[1,160,128]{2,1,0:T(8,128)(2,1)S(1)}, u32[]{:S(2)}, u32[]{:S(2)}) %collective-permute-start.11) | collective-permute-done | bytes 40992 | tf_op jit(solution)/shard_map/ppermute | solution.py:257
  74.4 0.1 collective-permute-done.10
  74.5 2.7 %collective-permute-done.12 = bf16[1,160,128]{2,1,0:T(8,128)(2,1)S(1)} collective-permute-done((bf16[1,160,128]{2,1,0:T(8,128)(2,1)S(1)}, bf16[1,160,128]{2,1,0:T(8,128)(2,1)S(1)}, u32[]{:S(2)}, u32[]{:S(2)}) %collective-permute-start.12) | collective-permute-done | bytes 40992 | tf_op jit(solution)/shard_map/ppermute | solution.py:257
  77.3 1.7 %collective-permute-start.13 = (bf16[1,160,128]{2,1,0:T(8,128)(2,1)S(1)}, bf16[1,160,128]{2,1,0:T(8,128)(2,1)S(1)}, u32[]{:S(2)}, u32[]{:S(2)}) collective-permute-start(bf16[1,160,128]{2,1,0:T(8,128)(2,1)S(1)} %get-tuple-element.51), channel_id=1, source_target_pairs={{0,64},{4,68},{64,0},{68,4},{128,192},{132,196},{192,128},{196,132... | collective-permute-start | bytes 122888 | tf_op jit(solution)/shard_map/ppermute | solution.py:257
  79.0 1.4 %collective-permute-done.13 = bf16[1,160,128]{2,1,0:T(8,128)(2,1)S(1)} collective-permute-done((bf16[1,160,128]{2,1,0:T(8,128)(2,1)S(1)}, bf16[1,160,128]{2,1,0:T(8,128)(2,1)S(1)}, u32[]{:S(2)}, u32[]{:S(2)}) %collective-permute-start.13) | collective-permute-done | bytes 40992 | tf_op jit(solution)/shard_map/ppermute | solution.py:257
  80.5 0.9 collective-permute-start.15
  81.3 3.6 %collective-permute-start.14 = (bf16[1,160,128]{2,1,0:T(8,128)(2,1)S(1)}, bf16[1,160,128]{2,1,0:T(8,128)(2,1)S(1)}, u32[]{:S(2)}, u32[]{:S(2)}) collective-permute-start(bf16[1,160,128]{2,1,0:T(8,128)(2,1)S(1)} %get-tuple-element.49), channel_id=1, source_target_pairs={{0,128},{4,132},{64,192},{68,196},{128,0},{132,4},{192,64},{196,68... | collective-permute-start | bytes 122888 | tf_op jit(solution)/shard_map/ppermute | solution.py:257
  84.9 1.3 %collective-permute-start.16 = (bf16[1,160,128]{2,1,0:T(8,128)(2,1)S(1)}, bf16[1,160,128]{2,1,0:T(8,128)(2,1)S(1)}, u32[]{:S(2)}, u32[]{:S(2)}) collective-permute-start(bf16[1,160,128]{2,1,0:T(8,128)(2,1)S(1)} %get-tuple-element.49), channel_id=1, source_target_pairs={{0,132},{4,128},{64,196},{68,192},{128,4},{132,0},{192,68},{196,64... | collective-permute-start | bytes 122888 | tf_op jit(solution)/shard_map/ppermute | solution.py:257
  86.2 1.1 %collective-permute-done.15 = bf16[1,160,128]{2,1,0:T(8,128)(2,1)S(1)} collective-permute-done((bf16[1,160,128]{2,1,0:T(8,128)(2,1)S(1)}, bf16[1,160,128]{2,1,0:T(8,128)(2,1)S(1)}, u32[]{:S(2)}, u32[]{:S(2)}) %collective-permute-start.15) | collective-permute-done | bytes 40992 | tf_op jit(solution)/shard_map/ppermute | solution.py:257
  87.4 0.0 collective-permute-done.14
  87.4 2.5 %collective-permute-done.16 = bf16[1,160,128]{2,1,0:T(8,128)(2,1)S(1)} collective-permute-done((bf16[1,160,128]{2,1,0:T(8,128)(2,1)S(1)}, bf16[1,160,128]{2,1,0:T(8,128)(2,1)S(1)}, u32[]{:S(2)}, u32[]{:S(2)}) %collective-permute-start.16) | collective-permute-done | bytes 40992 | tf_op jit(solution)/shard_map/ppermute | solution.py:257
  90.0 0.1 collective-permute-start.19
  90.1 1.4 %collective-permute-start.18 = (bf16[1,160,128]{2,1,0:T(8,128)(2,1)S(1)}, bf16[1,160,128]{2,1,0:T(8,128)(2,1)S(1)}, u32[]{:S(2)}, u32[]{:S(2)}) collective-permute-start(bf16[1,160,128]{2,1,0:T(8,128)(2,1)S(1)} %pad_maximum_fusion.10), channel_id=1, source_target_pairs={{0,2},{1,3},{2,0},{3,1},{4,6},{5,7},{6,4},{7,5},{8,10},{9,11},{10,... | collective-permute-start | bytes 122888 | tf_op jit(solution)/shard_map/ppermute | solution.py:257
  91.5 2.4 %collective-permute-start.17 = (bf16[1,160,128]{2,1,0:T(8,128)(2,1)S(1)}, bf16[1,160,128]{2,1,0:T(8,128)(2,1)S(1)}, u32[]{:S(2)}, u32[]{:S(2)}) collective-permute-start(bf16[1,160,128]{2,1,0:T(8,128)(2,1)S(1)} %pad_maximum_fusion.10), channel_id=1, source_target_pairs={{0,3},{1,2},{2,1},{3,0},{4,7},{5,6},{6,5},{7,4},{8,11},{9,10},{10,... | collective-permute-start | bytes 122888 | tf_op jit(solution)/shard_map/ppermute | solution.py:257
  93.9 0.0 collective-permute-done.19
  93.9 0.6 collective-permute-done.18
  94.5 1.3 %collective-permute-done.17 = bf16[1,160,128]{2,1,0:T(8,128)(2,1)S(1)} collective-permute-done((bf16[1,160,128]{2,1,0:T(8,128)(2,1)S(1)}, bf16[1,160,128]{2,1,0:T(8,128)(2,1)S(1)}, u32[]{:S(2)}, u32[]{:S(2)}) %collective-permute-start.17) | collective-permute-done | bytes 40992 | tf_op jit(solution)/shard_map/ppermute | solution.py:257
  95.9 7.3 %collective-permute-start.20 = (bf16[4,160,128]{2,1,0:T(8,128)(2,1)S(1)}, bf16[4,160,128]{2,1,0:T(8,128)(2,1)S(1)}, u32[]{:S(2)}, u32[]{:S(2)}) collective-permute-start(bf16[4,160,128]{2,1,0:T(8,128)(2,1)S(1)} %pad_maximum_fusion.6.mine), channel_id=1, source_target_pairs={{0,8},{8,0},{1,9},{9,1},{2,10},{10,2},{3,11},{11,3},{4,12},{12,4},... | collective-permute-start | bytes 491528 | tf_op jit(solution)/shard_map/ppermute | solution.py:257
  103.3 1.2 %pad_maximum_fusion = bf16[8,16,16,192]{3,2,1,0:T(8,128)(2,1)} fusion(bf16[8,16,8,192]{3,2,1,0:T(8,128)(2,1)S(1)} %get-tuple-element.18, bf16[8,16,8,192]{3,2,1,0:T(8,128)(2,1)S(1)} %get-tuple-element.17), kind=kLoop, calls=%fused_computation.13 | loop fusion | flops 1572864 | bytes 1572864 | tf_op jit(solution)/shard_map/concatenate | solution.py:422
  104.4 0.0 collective-permute-done.20.other
  104.4 0.9 unpack_sums.1
  (56 shorter events, 0.5 us)
Async XLA Ops:
  0.6 5.3 %copy-start.2 = (bf16[8,16,16,192]{3,2,1,0:T(8,128)(2,1)S(1)}, bf16[8,16,16,192]{3,2,1,0:T(8,128)(2,1)}, u32[]{:S(2)}) copy-start(bf16[8,16,16,192]{3,2,1,0:T(8,128)(2,1)} %param.8) | copy-start | bytes 2359300
  0.6 5.3 %copy-start.3 = (bf16[8,16,16,192]{3,2,1,0:T(8,128)(2,1)S(1)}, bf16[8,16,16,192]{3,2,1,0:T(8,128)(2,1)}, u32[]{:S(2)}) copy-start(bf16[8,16,16,192]{3,2,1,0:T(8,128)(2,1)} %param.7) | copy-start | bytes 2359300
  2.7 11.4 %collective-permute-start = (bf16[8,4,16,384]{3,2,1,0:T(8,128)(2,1)}, bf16[8,4,16,384]{3,2,1,0:T(8,128)(2,1)}, u32[]{:S(2)}, u32[]{:S(2)}) collective-permute-start(bf16[8,4,16,384]{3,2,1,0:T(8,128)(2,1)} %fusion.2), channel_id=1, source_target_pairs={{0,8},{8,0},{1,9},{9,1},{2,10},{10,2},{3,11},{11,3},{4,12},{12,4},... | collective-permute-start | bytes 1179656 | tf_op jit(solution)/shard_map/ppermute | solution.py:369
  6.9 18.4 %collective-permute-start.1 = (bf16[4,12,8,384]{3,2,1,0:T(8,128)(2,1)}, bf16[4,12,8,384]{3,2,1,0:T(8,128)(2,1)S(1)}, u32[]{:S(2)}, u32[]{:S(2)}) collective-permute-start(bf16[4,12,8,384]{3,2,1,0:T(8,128)(2,1)} %pad_maximum_fusion.3), channel_id=1, source_target_pairs={{0,240},{16,0},{32,16},{48,32},{64,48},{80,64},{96,80},{112,96},{1... | collective-permute-start | bytes 884744 | tf_op jit(solution)/shard_map/ppermute | solution.py:369
  11.8 1.8 %copy-start.5 = (f32[192]{0:T(256)S(1)}, f32[192]{0:T(256)}, u32[]{:S(2)}) copy-start(f32[192]{0:T(256)} %param.9) | copy-start | bytes 2308
  11.8 1.9 %copy-start.6 = (f32[192]{0:T(256)S(1)}, f32[192]{0:T(256)}, u32[]{:S(2)}) copy-start(f32[192]{0:T(256)} %param.10) | copy-start | bytes 2308
  11.8 2.1 %copy-start.4 = (f32[576]{0:T(1024)S(1)}, f32[576]{0:T(1024)}, u32[]{:S(2)}) copy-start(f32[576]{0:T(1024)} %param.12) | copy-start | bytes 6916
  11.8 2.2 %copy-start = (bf16[192,576]{1,0:T(8,128)(2,1)S(1)}, bf16[192,576]{1,0:T(8,128)(2,1)}, u32[]{:S(2)}) copy-start(bf16[192,576]{1,0:T(8,128)(2,1)} %w_rows.3) | copy-start | bytes 663556
  15.2 10.1 %collective-permute-start.2 = (bf16[4,4,8,384]{3,2,1,0:T(8,128)(2,1)S(1)}, bf16[4,4,8,384]{3,2,1,0:T(8,128)(2,1)S(1)}, u32[]{:S(2)}, u32[]{:S(2)}) collective-permute-start(bf16[4,4,8,384]{3,2,1,0:T(8,128)(2,1)S(1)} %slice.178), channel_id=1, source_target_pairs={{0,240},{16,0},{32,16},{48,32},{64,48},{80,64},{96,80},{112,96},{1... | collective-permute-start | bytes 294920 | tf_op jit(solution)/shard_map/ppermute | solution.py:369
  17.2 8.1 %copy-start.1 = (bf16[192,192]{1,0:T(8,128)(2,1)S(1)}, bf16[192,192]{1,0:T(8,128)(2,1)}, u32[]{:S(2)}) copy-start(bf16[192,192]{1,0:T(8,128)(2,1)} %proj.3) | copy-start | bytes 221188
  17.2 23.9 %collective-permute-start.4 = (bf16[4,16,4,384]{3,2,1,0:T(4,128)(2,1)S(1)}, bf16[4,16,4,384]{3,2,1,0:T(4,128)(2,1)S(1)}, u32[]{:S(2)}, u32[]{:S(2)}) collective-permute-start(bf16[4,16,4,384]{3,2,1,0:T(4,128)(2,1)S(1)} %get-tuple-element.37), channel_id=1, source_target_pairs={{0,240},{16,0},{32,16},{48,32},{64,48},{80,64},{96,80},{112,96},{1... | collective-permute-start | bytes 589832 | tf_op jit(solution)/shard_map/ppermute | solution.py:369
  17.5 23.4 %collective-permute-start.3 = (bf16[4,16,4,384]{3,2,1,0:T(4,128)(2,1)S(1)}, bf16[4,16,4,384]{3,2,1,0:T(4,128)(2,1)S(1)}, u32[]{:S(2)}, u32[]{:S(2)}) collective-permute-start(bf16[4,16,4,384]{3,2,1,0:T(4,128)(2,1)S(1)} %get-tuple-element.39), channel_id=1, source_target_pairs={{0,7},{1,0},{2,1},{3,2},{4,3},{5,4},{6,5},{7,6},{8,15},{9,8},{10,9... | collective-permute-start | bytes 589832 | tf_op jit(solution)/shard_map/ppermute | solution.py:369
  24.2 16.9 %collective-permute-start.5 = (bf16[4,16,4,384]{3,2,1,0:T(4,128)(2,1)S(1)}, bf16[4,16,4,384]{3,2,1,0:T(4,128)(2,1)S(1)}, u32[]{:S(2)}, u32[]{:S(2)}) collective-permute-start(bf16[4,16,4,384]{3,2,1,0:T(4,128)(2,1)S(1)} %get-tuple-element.40), channel_id=1, source_target_pairs={{0,247},{1,240},{2,241},{3,242},{4,243},{5,244},{6,245},{7,246},{1... | collective-permute-start | bytes 589832 | tf_op jit(solution)/shard_map/ppermute | solution.py:379
  54.9 2.0 %collective-permute-start.6 = (bf16[4,160,128]{2,1,0:T(8,128)(2,1)S(1)}, bf16[4,160,128]{2,1,0:T(8,128)(2,1)S(1)}, u32[]{:S(2)}, u32[]{:S(2)}) collective-permute-start(bf16[4,160,128]{2,1,0:T(8,128)(2,1)S(1)} %pad_maximum_fusion.5), channel_id=1, source_target_pairs={{0,8},{8,0},{1,9},{9,1},{2,10},{10,2},{3,11},{11,3},{4,12},{12,4},... | collective-permute-start | bytes 491528 | tf_op jit(solution)/shard_map/ppermute | solution.py:257
  57.1 8.7 %collective-permute-start.7 = (bf16[1,160,128]{2,1,0:T(8,128)(2,1)S(1)}, bf16[1,160,128]{2,1,0:T(8,128)(2,1)S(1)}, u32[]{:S(2)}, u32[]{:S(2)}) collective-permute-start(bf16[1,160,128]{2,1,0:T(8,128)(2,1)S(1)} %get-tuple-element.45), channel_id=1, source_target_pairs={{0,2},{1,3},{2,0},{3,1},{4,6},{5,7},{6,4},{7,5},{8,10},{9,11},{10,... | collective-permute-start | bytes 122888 | tf_op jit(solution)/shard_map/ppermute | solution.py:257
  57.2 10.5 %collective-permute-start.8 = (bf16[1,160,128]{2,1,0:T(8,128)(2,1)S(1)}, bf16[1,160,128]{2,1,0:T(8,128)(2,1)S(1)}, u32[]{:S(2)}, u32[]{:S(2)}) collective-permute-start(bf16[1,160,128]{2,1,0:T(8,128)(2,1)S(1)} %get-tuple-element.46), channel_id=1, source_target_pairs={{0,1},{1,0},{2,3},{3,2},{4,5},{5,4},{6,7},{7,6},{8,9},{9,8},{10,11... | collective-permute-start | bytes 122888 | tf_op jit(solution)/shard_map/ppermute | solution.py:257
  65.8 4.1 %collective-permute-start.9 = (bf16[1,160,128]{2,1,0:T(8,128)(2,1)S(1)}, bf16[1,160,128]{2,1,0:T(8,128)(2,1)S(1)}, u32[]{:S(2)}, u32[]{:S(2)}) collective-permute-start(bf16[1,160,128]{2,1,0:T(8,128)(2,1)S(1)} %get-tuple-element.47), channel_id=1, source_target_pairs={{0,3},{1,2},{2,1},{3,0},{4,7},{5,6},{6,5},{7,4},{8,11},{9,10},{10,... | collective-permute-start | bytes 122888 | tf_op jit(solution)/shard_map/ppermute | solution.py:257
  69.9 4.4 %collective-permute-start.11 = (bf16[1,160,128]{2,1,0:T(8,128)(2,1)S(1)}, bf16[1,160,128]{2,1,0:T(8,128)(2,1)S(1)}, u32[]{:S(2)}, u32[]{:S(2)}) collective-permute-start(bf16[1,160,128]{2,1,0:T(8,128)(2,1)S(1)} %get-tuple-element.53), channel_id=1, source_target_pairs={{0,32},{16,48},{32,0},{48,16},{1,33},{17,49},{33,1},{49,17},{2,34}... | collective-permute-start | bytes 122888 | tf_op jit(solution)/shard_map/ppermute | solution.py:257
  70.0 4.5 %collective-permute-start.10 = (bf16[1,160,128]{2,1,0:T(8,128)(2,1)S(1)}, bf16[1,160,128]{2,1,0:T(8,128)(2,1)S(1)}, u32[]{:S(2)}, u32[]{:S(2)}) collective-permute-start(bf16[1,160,128]{2,1,0:T(8,128)(2,1)S(1)} %get-tuple-element.53), channel_id=1, source_target_pairs={{0,16},{16,0},{32,48},{48,32},{1,17},{17,1},{33,49},{49,33},{2,18}... | collective-permute-start | bytes 122888 | tf_op jit(solution)/shard_map/ppermute | solution.py:257
  72.7 4.5 %collective-permute-start.12 = (bf16[1,160,128]{2,1,0:T(8,128)(2,1)S(1)}, bf16[1,160,128]{2,1,0:T(8,128)(2,1)S(1)}, u32[]{:S(2)}, u32[]{:S(2)}) collective-permute-start(bf16[1,160,128]{2,1,0:T(8,128)(2,1)S(1)} %get-tuple-element.53), channel_id=1, source_target_pairs={{0,48},{16,32},{32,16},{48,0},{1,49},{17,33},{33,17},{49,1},{2,50}... | collective-permute-start | bytes 122888 | tf_op jit(solution)/shard_map/ppermute | solution.py:257
  77.3 3.1 %collective-permute-start.13 = (bf16[1,160,128]{2,1,0:T(8,128)(2,1)S(1)}, bf16[1,160,128]{2,1,0:T(8,128)(2,1)S(1)}, u32[]{:S(2)}, u32[]{:S(2)}) collective-permute-start(bf16[1,160,128]{2,1,0:T(8,128)(2,1)S(1)} %get-tuple-element.51), channel_id=1, source_target_pairs={{0,64},{4,68},{64,0},{68,4},{128,192},{132,196},{192,128},{196,132... | collective-permute-start | bytes 122888 | tf_op jit(solution)/shard_map/ppermute | solution.py:257
  80.5 6.8 %collective-permute-start.15 = (bf16[1,160,128]{2,1,0:T(8,128)(2,1)S(1)}, bf16[1,160,128]{2,1,0:T(8,128)(2,1)S(1)}, u32[]{:S(2)}, u32[]{:S(2)}) collective-permute-start(bf16[1,160,128]{2,1,0:T(8,128)(2,1)S(1)} %get-tuple-element.49), channel_id=1, source_target_pairs={{0,4},{4,0},{64,68},{68,64},{128,132},{132,128},{192,196},{196,192... | collective-permute-start | bytes 122888 | tf_op jit(solution)/shard_map/ppermute | solution.py:257
  81.3 6.0 %collective-permute-start.14 = (bf16[1,160,128]{2,1,0:T(8,128)(2,1)S(1)}, bf16[1,160,128]{2,1,0:T(8,128)(2,1)S(1)}, u32[]{:S(2)}, u32[]{:S(2)}) collective-permute-start(bf16[1,160,128]{2,1,0:T(8,128)(2,1)S(1)} %get-tuple-element.49), channel_id=1, source_target_pairs={{0,128},{4,132},{64,192},{68,196},{128,0},{132,4},{192,64},{196,68... | collective-permute-start | bytes 122888 | tf_op jit(solution)/shard_map/ppermute | solution.py:257
  84.9 5.0 %collective-permute-start.16 = (bf16[1,160,128]{2,1,0:T(8,128)(2,1)S(1)}, bf16[1,160,128]{2,1,0:T(8,128)(2,1)S(1)}, u32[]{:S(2)}, u32[]{:S(2)}) collective-permute-start(bf16[1,160,128]{2,1,0:T(8,128)(2,1)S(1)} %get-tuple-element.49), channel_id=1, source_target_pairs={{0,132},{4,128},{64,196},{68,192},{128,4},{132,0},{192,68},{196,64... | collective-permute-start | bytes 122888 | tf_op jit(solution)/shard_map/ppermute | solution.py:257
  90.0 3.9 %collective-permute-start.19 = (bf16[1,160,128]{2,1,0:T(8,128)(2,1)S(1)}, bf16[1,160,128]{2,1,0:T(8,128)(2,1)S(1)}, u32[]{:S(2)}, u32[]{:S(2)}) collective-permute-start(bf16[1,160,128]{2,1,0:T(8,128)(2,1)S(1)} %pad_maximum_fusion.10), channel_id=1, source_target_pairs={{0,1},{1,0},{2,3},{3,2},{4,5},{5,4},{6,7},{7,6},{8,9},{9,8},{10,11... | collective-permute-start | bytes 122888 | tf_op jit(solution)/shard_map/ppermute | solution.py:257
  90.1 4.4 %collective-permute-start.18 = (bf16[1,160,128]{2,1,0:T(8,128)(2,1)S(1)}, bf16[1,160,128]{2,1,0:T(8,128)(2,1)S(1)}, u32[]{:S(2)}, u32[]{:S(2)}) collective-permute-start(bf16[1,160,128]{2,1,0:T(8,128)(2,1)S(1)} %pad_maximum_fusion.10), channel_id=1, source_target_pairs={{0,2},{1,3},{2,0},{3,1},{4,6},{5,7},{6,4},{7,5},{8,10},{9,11},{10,... | collective-permute-start | bytes 122888 | tf_op jit(solution)/shard_map/ppermute | solution.py:257
  91.5 4.4 %collective-permute-start.17 = (bf16[1,160,128]{2,1,0:T(8,128)(2,1)S(1)}, bf16[1,160,128]{2,1,0:T(8,128)(2,1)S(1)}, u32[]{:S(2)}, u32[]{:S(2)}) collective-permute-start(bf16[1,160,128]{2,1,0:T(8,128)(2,1)S(1)} %pad_maximum_fusion.10), channel_id=1, source_target_pairs={{0,3},{1,2},{2,1},{3,0},{4,7},{5,6},{6,5},{7,4},{8,11},{9,10},{10,... | collective-permute-start | bytes 122888 | tf_op jit(solution)/shard_map/ppermute | solution.py:257
  95.9 8.5 %collective-permute-start.20 = (bf16[4,160,128]{2,1,0:T(8,128)(2,1)S(1)}, bf16[4,160,128]{2,1,0:T(8,128)(2,1)S(1)}, u32[]{:S(2)}, u32[]{:S(2)}) collective-permute-start(bf16[4,160,128]{2,1,0:T(8,128)(2,1)S(1)} %pad_maximum_fusion.6.mine), channel_id=1, source_target_pairs={{0,8},{8,0},{1,9},{9,1},{2,10},{10,2},{3,11},{11,3},{4,12},{12,4},... | collective-permute-start | bytes 491528 | tf_op jit(solution)/shard_map/ppermute | solution.py:257
